TPU v7x, 256 devices: a whole 4x4x8 slice. The times are simulated.
256 devices in a mesh: tile: 64 (over z_hi, x, y, core), lev: 4 (over z_lo).
Axes of the slice: x: 4, y: 4, z: 8 (z_hi: 2, z_lo: 4; z = z_hi * 4 + z_lo), core: 2. Of those that a mesh axis runs over, the one named last changes fastest.
Arguments:
- tracers: float32 [64, 8, 8, 72, 128], P('tile', None, None, 'lev'), may hold values from -6 to 6
- courant_first: float32 [64, 8, 8, 72], P('tile', None, None, 'lev'), may hold values from -0.9 to 0.9
- courant_second: float32 [64, 8, 8, 72], P('tile', None, None, 'lev'), may hold values from -0.9 to 0.9
- weights: float32 [64, 8, 8, 72, 72], P('tile', 'lev'), may hold values from 0.05 to 1
- frame_flip: int32 [64, 2], P('tile'), may hold values from 0 to 1
Outputs:
- transported: float32 [64, 8, 8, 72, 128], P('tile', None, None, 'lev')
All inputs are finite; a program needn't handle non-finite values.
Results may differ from a plain program's by a relative error of at most 0.0003.
Values sent between devices are 32-bit elements; how exact they have to be, the bound alone decides.
A program may use at most 64 MiB of HBM per device.

v0:
```python
import jax
import jax.numpy as jnp
from jax import lax
from jax.sharding import PartitionSpec as P

SUBSTEPS = 3


def passed_along(value, axis, steps):
    count = lax.axis_size(axis)
    pairs = [(source, (source + steps) % count) for source in range(count)]
    return lax.ppermute(value, axis, pairs)


def ppm_update(extended, courant, along):
    length = extended.shape[along] - 6

    def window(values, offset, amount):
        return lax.slice_in_dim(values, offset, offset + amount, axis=along)

    interfaces = (
        7.0 * (window(extended, 1, length + 3) + window(extended, 2, length + 3))
        - (window(extended, 0, length + 3) + window(extended, 3, length + 3))
    ) / 12.0
    low_edge = window(interfaces, 0, length + 2)
    high_edge = window(interfaces, 1, length + 2)
    centre = window(extended, 2, length + 2)
    gradient = high_edge - low_edge
    curvature = 6.0 * centre - 3.0 * (low_edge + high_edge)
    upward = courant * (
        window(high_edge, 0, length + 1)
        - 0.5
        * courant
        * (
            window(gradient, 0, length + 1)
            - (1.0 - courant * (2.0 / 3.0)) * window(curvature, 0, length + 1)
        )
    )
    downward = courant * (
        window(low_edge, 1, length + 1)
        - 0.5
        * courant
        * (
            window(gradient, 1, length + 1)
            + (1.0 + courant * (2.0 / 3.0)) * window(curvature, 1, length + 1)
        )
    )
    fluxes = jnp.where(courant >= 0.0, upward, downward)
    return window(centre, 1, length) - (window(fluxes, 1, length) - window(fluxes, 0, length))


def to_frame(blocks, flip_flags):
    first_flag = (flip_flags[:, 0] == 1)[:, None, None, None, None]
    second_flag = (flip_flags[:, 1] == 1)[:, None, None, None, None]
    turned = jnp.where(first_flag, blocks[:, ::-1], blocks)
    return jnp.where(second_flag, turned[:, :, ::-1], turned)


def mixing_matrix(weights):
    totals = jnp.sum(weights, axis=-1, keepdims=True)
    identity = jnp.eye(weights.shape[-1], dtype=jnp.float32)
    return 0.6 * identity + 0.4 * (weights / totals)


def on_device(tracers, courant_first, courant_second, weights, frame_flip):
    stride = max(2, lax.axis_size("tile") // 8)
    extent = tracers.shape[1]
    fields = to_frame(tracers, frame_flip)
    first_faces = courant_first[..., None]
    second_faces = courant_second[..., None]

    def swap_columns(low_columns, high_columns):
        from_low, low_faces = passed_along(
            (high_columns, second_faces[:, :, extent - 1 :]), "tile", 1
        )
        from_high = passed_along(low_columns, "tile", -1)
        return (from_low, low_faces, from_high)

    def sweep_second(values, margins):
        from_low, low_faces, from_high = margins
        extended = jnp.concatenate([from_low, values, from_high], axis=2)
        courant = jnp.concatenate([low_faces, second_faces], axis=2)
        return ppm_update(extended, courant, 2)

    for substep in range(SUBSTEPS):
        swap_from_low, swap_low_faces = passed_along(
            (fields[:, extent - 3 :], first_faces[:, extent - 1 :]), "tile", stride
        )
        swap_from_high = passed_along(fields[:, :3], "tile", -stride)
        sweep_extended = jnp.concatenate([swap_from_low, fields, swap_from_high], axis=1)
        sweep_courant = jnp.concatenate([swap_low_faces, first_faces], axis=1)
        fields = ppm_update(sweep_extended, sweep_courant, 1)
        fields = sweep_second(fields, swap_columns(fields[:, :, :3], fields[:, :, extent - 3 :]))
    advected = to_frame(fields, frame_flip)
    mixing = mixing_matrix(weights)
    columns = lax.all_to_all(advected, "lev", split_axis=1, concat_axis=3, tiled=True)
    mixed = jnp.einsum("txykl,txylq->txykq", mixing, columns, precision=lax.Precision.HIGHEST)
    result = lax.all_to_all(mixed, "lev", split_axis=3, concat_axis=1, tiled=True)
    return result


def solution(mesh):
    in_specs = (
        P("tile", None, None, "lev", None),
        P("tile", None, None, "lev"),
        P("tile", None, None, "lev"),
        P("tile", "lev", None, None, None),
        P("tile", None),
    )
    out_specs = P("tile", None, None, "lev", None)
    return jax.shard_map(
        on_device, mesh=mesh, in_specs=in_specs, out_specs=out_specs, check_vma=False
    )
```

profile of v0, /device:TPU:31, one launch (start us, length us, event | category | flops | bytes accessed | tf_op | source)
XLA Modules:
  0.0 165.2 jit_solution(15162871919754180910)
XLA Ops:
  0.0 0.7 slice.412
  0.7 6.8 %collective-permute-start = (f32[1,1,8,18,1]{3,2,4,1,0:T(8,128)S(1)}, f32[1,1,8,18,1]{3,2,4,1,0:T(8,128)S(1)}, u32[]{:S(2)}, u32[]{:S(2)}) collective-permute-start(f32[1,1,8,18,1]{3,2,4,1,0:T(8,128)S(1)} %slice.412), channel_id=1, source_target_pairs={{0,32},{4,36},{8,40},{12,44},{16,48},{20,52},{24,56},{28,60},{32,6... | collective-permute-start | bytes 1736 | tf_op jit(solution)/shard_map/ppermute | solution.py:12
  7.5 1.3 fusion.100
  9.5 1.4 reverse_select_fusion.1
  10.8 0.3 rev.13
  11.9 1.3 collective-permute-start.1
  13.2 0.3 collective-permute-start.2
  13.5 8.4 %collective-permute-start.3 = (f32[1,8,1,18,1]{3,1,4,2,0:T(8,128)S(1)}, f32[1,8,1,18,1]{3,1,4,2,0:T(8,128)S(1)}, u32[]{:S(2)}, u32[]{:S(2)}) collective-permute-start(f32[1,8,1,18,1]{3,1,4,2,0:T(8,128)S(1)} %bitcast.49), channel_id=1, source_target_pairs={{0,4},{4,8},{8,12},{12,16},{16,20},{20,24},{24,28},{28,32},{32,36}... | collective-permute-start | bytes 1736 | tf_op jit(solution)/shard_map/ppermute | solution.py:12
  23.1 1.9 %collective-permute-done.2 = f32[1,3,8,18,128]{4,2,3,0,1:T(8,128)S(1)} collective-permute-done((f32[1,3,8,18,128]{4,2,3,0,1:T(8,128)S(1)}, f32[1,3,8,18,128]{4,2,3,0,1:T(8,128)S(1)}, u32[]{:S(2)}, u32[]{:S(2)}) %collective-permute-start.2) | collective-permute-done | bytes 221216 | tf_op jit(solution)/shard_map/ppermute | solution.py:12
  25.1 0.2 fusion.47
  25.4 1.1 fusion.73
  26.7 8.6 %collective-permute-start.4 = (f32[1,8,3,18,128]{4,2,3,0,1:T(4,128)S(1)}, f32[1,8,3,18,128]{4,2,3,0,1:T(4,128)S(1)}, u32[]{:S(2)}, u32[]{:S(2)}) collective-permute-start(f32[1,8,3,18,128]{4,2,3,0,1:T(4,128)S(1)} %get-tuple-element.25), channel_id=1, source_target_pairs={{0,4},{4,8},{8,12},{12,16},{16,20},{20,24},{24,28},{28,32},{32,36}... | collective-permute-start | bytes 663560 | tf_op jit(solution)/shard_map/ppermute | solution.py:12
  35.7 6.4 %collective-permute-done.4 = f32[1,8,3,18,128]{4,2,3,0,1:T(4,128)S(1)} collective-permute-done((f32[1,8,3,18,128]{4,2,3,0,1:T(4,128)S(1)}, f32[1,8,3,18,128]{4,2,3,0,1:T(4,128)S(1)}, u32[]{:S(2)}, u32[]{:S(2)}) %collective-permute-start.4) | collective-permute-done | bytes 221216 | tf_op jit(solution)/shard_map/ppermute | solution.py:12
  42.1 7.6 %collective-permute-done.5 = f32[1,8,3,18,128]{4,2,3,0,1:T(4,128)S(1)} collective-permute-done((f32[1,8,3,18,128]{4,2,3,0,1:T(4,128)S(1)}, f32[1,8,3,18,128]{4,2,3,0,1:T(4,128)S(1)}, u32[]{:S(2)}, u32[]{:S(2)}) %collective-permute-start.5) | collective-permute-done | bytes 221216 | tf_op jit(solution)/shard_map/ppermute | solution.py:12
  49.7 0.2 pad_maximum_fusion
  49.9 0.5 fusion.38
  50.4 0.3 slice_subtract_fusion.2
  50.8 2.1 %fusion.30 = f32[1,8,9,18,128]{4,2,3,0,1:T(8,128)S(1)} fusion(f32[1,8,10,18,128]{4,2,3,0,1:T(8,128)S(1)} %get-tuple-element.10, f32[1,8,10,18,128]{4,2,3,0,1:T(8,128)S(1)} %get-tuple-element.9, f32[1,8,11,18,128]{4,2,3,0,1:T(8,128)S(1)} %fusion.38, f32[8,9,18]{1,2,0:T(8,128)S(1)} %copy.78, f32[8,9,18]{1,2,0:T(8,128)S(1)} %copy.77, f32[8,9,18]{1,2,0:T(8,128)S(1)} %copy.76, ...), kind=kLoop, calls=%fused_computation.40 | loop fusion | flops 1824768 | bytes 4003344 | tf_op jit(solution)/shard_map/jit(_where)/select_n | solution.py:48
  53.2 1.5 collective-permute-start.7
  54.6 3.3 %collective-permute-done.6 = f32[1,3,8,18,128]{4,2,3,0,1:T(8,128)S(1)} collective-permute-done((f32[1,3,8,18,128]{4,2,3,0,1:T(8,128)S(1)}, f32[1,3,8,18,128]{4,2,3,0,1:T(8,128)S(1)}, u32[]{:S(2)}, u32[]{:S(2)}) %collective-permute-start.6) | collective-permute-done | bytes 221216 | tf_op jit(solution)/shard_map/ppermute | solution.py:12
  57.9 6.1 %collective-permute-done.7 = f32[1,3,8,18,128]{4,2,3,0,1:T(8,128)S(1)} collective-permute-done((f32[1,3,8,18,128]{4,2,3,0,1:T(8,128)S(1)}, f32[1,3,8,18,128]{4,2,3,0,1:T(8,128)S(1)}, u32[]{:S(2)}, u32[]{:S(2)}) %collective-permute-start.7) | collective-permute-done | bytes 221216 | tf_op jit(solution)/shard_map/ppermute | solution.py:12
  64.4 1.1 fusion.64
  65.7 4.3 %collective-permute-start.8 = (f32[1,8,3,18,128]{4,2,3,0,1:T(4,128)S(1)}, f32[1,8,3,18,128]{4,2,3,0,1:T(4,128)S(1)}, u32[]{:S(2)}, u32[]{:S(2)}) collective-permute-start(f32[1,8,3,18,128]{4,2,3,0,1:T(4,128)S(1)} %get-tuple-element.21), channel_id=1, source_target_pairs={{0,4},{4,8},{8,12},{12,16},{16,20},{20,24},{24,28},{28,32},{32,36}... | collective-permute-start | bytes 663560 | tf_op jit(solution)/shard_map/ppermute | solution.py:12
  70.0 5.0 %collective-permute-done.8 = f32[1,8,3,18,128]{4,2,3,0,1:T(4,128)S(1)} collective-permute-done((f32[1,8,3,18,128]{4,2,3,0,1:T(4,128)S(1)}, f32[1,8,3,18,128]{4,2,3,0,1:T(4,128)S(1)}, u32[]{:S(2)}, u32[]{:S(2)}) %collective-permute-start.8) | collective-permute-done | bytes 221216 | tf_op jit(solution)/shard_map/ppermute | solution.py:12
  75.0 15.3 %collective-permute-done.9 = f32[1,8,3,18,128]{4,2,3,0,1:T(4,128)S(1)} collective-permute-done((f32[1,8,3,18,128]{4,2,3,0,1:T(4,128)S(1)}, f32[1,8,3,18,128]{4,2,3,0,1:T(4,128)S(1)}, u32[]{:S(2)}, u32[]{:S(2)}) %collective-permute-start.9) | collective-permute-done | bytes 221216 | tf_op jit(solution)/shard_map/ppermute | solution.py:12
  90.3 0.2 pad_maximum_fusion.1
  90.5 0.5 fusion.25
  91.0 0.3 slice_subtract_fusion.1
  91.4 2.1 %fusion.17 = f32[1,8,9,18,128]{4,2,3,0,1:T(8,128)S(1)} fusion(f32[1,8,10,18,128]{4,2,3,0,1:T(8,128)S(1)} %get-tuple-element.8, f32[1,8,10,18,128]{4,2,3,0,1:T(8,128)S(1)} %get-tuple-element.7, f32[1,8,11,18,128]{4,2,3,0,1:T(8,128)S(1)} %fusion.25, f32[8,9,18]{1,2,0:T(8,128)S(1)} %copy.78, f32[8,9,18]{1,2,0:T(8,128)S(1)} %copy.77, f32[8,9,18]{1,2,0:T(8,128)S(1)} %copy.76, ...), kind=kLoop, calls=%fused_computation.23 | loop fusion | flops 1824768 | bytes 4003344 | tf_op jit(solution)/shard_map/jit(_where)/select_n | solution.py:48
  93.7 1.5 collective-permute-start.11
  95.1 3.3 %collective-permute-done.10 = f32[1,3,8,18,128]{4,2,3,0,1:T(8,128)S(1)} collective-permute-done((f32[1,3,8,18,128]{4,2,3,0,1:T(8,128)S(1)}, f32[1,3,8,18,128]{4,2,3,0,1:T(8,128)S(1)}, u32[]{:S(2)}, u32[]{:S(2)}) %collective-permute-start.10) | collective-permute-done | bytes 221216 | tf_op jit(solution)/shard_map/ppermute | solution.py:12
  98.5 6.2 %collective-permute-done.11 = f32[1,3,8,18,128]{4,2,3,0,1:T(8,128)S(1)} collective-permute-done((f32[1,3,8,18,128]{4,2,3,0,1:T(8,128)S(1)}, f32[1,3,8,18,128]{4,2,3,0,1:T(8,128)S(1)}, u32[]{:S(2)}, u32[]{:S(2)}) %collective-permute-start.11) | collective-permute-done | bytes 221216 | tf_op jit(solution)/shard_map/ppermute | solution.py:12
  105.0 1.1 fusion.55
  106.4 2.5 %collective-permute-start.12 = (f32[1,8,3,18,128]{4,2,3,0,1:T(4,128)S(1)}, f32[1,8,3,18,128]{4,2,3,0,1:T(4,128)S(1)}, u32[]{:S(2)}, u32[]{:S(2)}) collective-permute-start(f32[1,8,3,18,128]{4,2,3,0,1:T(4,128)S(1)} %get-tuple-element.17), channel_id=1, source_target_pairs={{0,4},{4,8},{8,12},{12,16},{16,20},{20,24},{24,28},{28,32},{32,36}... | collective-permute-start | bytes 663560 | tf_op jit(solution)/shard_map/ppermute | solution.py:12
  108.9 4.6 %collective-permute-done.12 = f32[1,8,3,18,128]{4,2,3,0,1:T(4,128)S(1)} collective-permute-done((f32[1,8,3,18,128]{4,2,3,0,1:T(4,128)S(1)}, f32[1,8,3,18,128]{4,2,3,0,1:T(4,128)S(1)}, u32[]{:S(2)}, u32[]{:S(2)}) %collective-permute-start.12) | collective-permute-done | bytes 221216 | tf_op jit(solution)/shard_map/ppermute | solution.py:12
  113.4 13.8 %collective-permute-done.13 = f32[1,8,3,18,128]{4,2,3,0,1:T(4,128)S(1)} collective-permute-done((f32[1,8,3,18,128]{4,2,3,0,1:T(4,128)S(1)}, f32[1,8,3,18,128]{4,2,3,0,1:T(4,128)S(1)}, u32[]{:S(2)}, u32[]{:S(2)}) %collective-permute-start.13) | collective-permute-done | bytes 221216 | tf_op jit(solution)/shard_map/ppermute | solution.py:12
  127.2 0.2 pad_maximum_fusion.2
  127.5 0.5 fusion.12
  128.0 0.3 slice_subtract_fusion
  128.3 2.1 %fusion.4 = f32[1,8,9,18,128]{4,2,3,0,1:T(8,128)S(1)} fusion(f32[1,8,10,18,128]{4,2,3,0,1:T(8,128)S(1)} %get-tuple-element.6, f32[1,8,10,18,128]{4,2,3,0,1:T(8,128)S(1)} %get-tuple-element.5, f32[1,8,11,18,128]{4,2,3,0,1:T(8,128)S(1)} %fusion.12, f32[8,9,18]{1,2,0:T(8,128)S(1)} %copy.78, f32[8,9,18]{1,2,0:T(8,128)S(1)} %copy.77, f32[8,9,18]{1,2,0:T(8,128)S(1)} %copy.76, ...), kind=kLoop, calls=%fused_computation.6 | loop fusion | flops 1824768 | bytes 4003344 | tf_op jit(solution)/shard_map/jit(_where)/select_n | solution.py:48
  130.6 0.3 rev.15
  130.9 0.9 broadcast_select_fusion
  131.8 3.5 %all-to-all-start = ((f32[1,8,8,18,128]{4,2,3,0,1:T(8,128)}), f32[1,8,8,18,128]{4,2,3,0,1:T(8,128)S(1)}, u32[]{:S(2)}, u32[]{:S(2)}) async-start(f32[1,8,8,18,128]{4,2,3,0,1:T(8,128)} %broadcast_select_fusion), calls=%async_computation | async-start | bytes 1179648 | tf_op jit(solution)/shard_map/all_to_all | solution.py:96
  135.3 0.3 reduce_sum.9
  135.6 14.9 %all-to-all-done = f32[1,8,8,18,128]{4,2,3,0,1:T(8,128)S(1)} async-done(((f32[1,8,8,18,128]{4,2,3,0,1:T(8,128)}), f32[1,8,8,18,128]{4,2,3,0,1:T(8,128)S(1)}, u32[]{:S(2)}, u32[]{:S(2)}) %all-to-all-start) | async-done | bytes 589856 | tf_op jit(solution)/shard_map/all_to_all | solution.py:96
  150.6 1.2 convolution_bitcast_fusion
  152.0 12.3 %all_to_all.33 = f32[1,2,8,72,128]{4,2,1,0,3:T(8,128)S(1)} all-to-all(f32[1,2,8,72,128]{4,2,1,0,3:T(8,128)S(1)} %copy.81), channel_id=1, replica_groups=mesh['tile'=64,'lev'=4] {'lev'}, dimensions={3} | all-to-all | bytes 1179648 | tf_op jit(solution)/shard_map/all_to_all | solution.py:98
  164.3 0.9 copy.83
  (60 shorter events, 3.8 us)
Async XLA Ops:
  0.7 21.2 %collective-permute-start = (f32[1,1,8,18,1]{3,2,4,1,0:T(8,128)S(1)}, f32[1,1,8,18,1]{3,2,4,1,0:T(8,128)S(1)}, u32[]{:S(2)}, u32[]{:S(2)}) collective-permute-start(f32[1,1,8,18,1]{3,2,4,1,0:T(8,128)S(1)} %slice.412), channel_id=1, source_target_pairs={{0,32},{4,36},{8,40},{12,44},{16,48},{20,52},{24,56},{28,60},{32,6... | collective-permute-start | bytes 1736 | tf_op jit(solution)/shard_map/ppermute | solution.py:12
  9.5 2.3 %copy-start = (f32[1,8,8,18,128]{4,2,3,1,0:T(8,128)S(1)}, f32[1,8,8,18,128]{4,2,3,1,0:T(8,128)}, u32[]{:S(2)}) copy-start(f32[1,8,8,18,128]{4,2,3,1,0:T(8,128)} %param.5) | copy-start | bytes 1769476
  11.8 1.7 %copy-start.3 = (f32[1,8,8,18]{3,2,1,0:T(8,128)S(1)}, f32[1,8,8,18]{3,2,1,0:T(8,128)}, u32[]{:S(2)}) copy-start(f32[1,8,8,18]{3,2,1,0:T(8,128)} %param.7) | copy-start | bytes 13828
  11.8 10.1 %copy-start.2 = (f32[1,8,8,18]{3,2,1,0:T(8,128)S(1)}, f32[1,8,8,18]{3,2,1,0:T(8,128)}, u32[]{:S(2)}) copy-start(f32[1,8,8,18]{3,2,1,0:T(8,128)} %param.6) | copy-start | bytes 13828
  11.9 11.2 %collective-permute-start.1 = (f32[1,3,8,18,128]{4,2,3,0,1:T(8,128)S(1)}, f32[1,3,8,18,128]{4,2,3,0,1:T(8,128)S(1)}, u32[]{:S(2)}, u32[]{:S(2)}) collective-permute-start(f32[1,3,8,18,128]{4,2,3,0,1:T(8,128)S(1)} %get-tuple-element.27), channel_id=1, source_target_pairs={{0,32},{4,36},{8,40},{12,44},{16,48},{20,52},{24,56},{28,60},{32,6... | collective-permute-start | bytes 663560 | tf_op jit(solution)/shard_map/ppermute | solution.py:12
  13.2 11.8 %collective-permute-start.2 = (f32[1,3,8,18,128]{4,2,3,0,1:T(8,128)S(1)}, f32[1,3,8,18,128]{4,2,3,0,1:T(8,128)S(1)}, u32[]{:S(2)}, u32[]{:S(2)}) collective-permute-start(f32[1,3,8,18,128]{4,2,3,0,1:T(8,128)S(1)} %get-tuple-element.28), channel_id=1, source_target_pairs={{0,224},{4,228},{8,232},{12,236},{16,240},{20,244},{24,248},{28,25... | collective-permute-start | bytes 663560 | tf_op jit(solution)/shard_map/ppermute | solution.py:12
  13.5 9.1 %collective-permute-start.3 = (f32[1,8,1,18,1]{3,1,4,2,0:T(8,128)S(1)}, f32[1,8,1,18,1]{3,1,4,2,0:T(8,128)S(1)}, u32[]{:S(2)}, u32[]{:S(2)}) collective-permute-start(f32[1,8,1,18,1]{3,1,4,2,0:T(8,128)S(1)} %bitcast.49), channel_id=1, source_target_pairs={{0,4},{4,8},{8,12},{12,16},{16,20},{20,24},{24,28},{28,32},{32,36}... | collective-permute-start | bytes 1736 | tf_op jit(solution)/shard_map/ppermute | solution.py:12
  26.7 15.4 %collective-permute-start.4 = (f32[1,8,3,18,128]{4,2,3,0,1:T(4,128)S(1)}, f32[1,8,3,18,128]{4,2,3,0,1:T(4,128)S(1)}, u32[]{:S(2)}, u32[]{:S(2)}) collective-permute-start(f32[1,8,3,18,128]{4,2,3,0,1:T(4,128)S(1)} %get-tuple-element.25), channel_id=1, source_target_pairs={{0,4},{4,8},{8,12},{12,16},{16,20},{20,24},{24,28},{28,32},{32,36}... | collective-permute-start | bytes 663560 | tf_op jit(solution)/shard_map/ppermute | solution.py:12
  35.3 14.4 %collective-permute-start.5 = (f32[1,8,3,18,128]{4,2,3,0,1:T(4,128)S(1)}, f32[1,8,3,18,128]{4,2,3,0,1:T(4,128)S(1)}, u32[]{:S(2)}, u32[]{:S(2)}) collective-permute-start(f32[1,8,3,18,128]{4,2,3,0,1:T(4,128)S(1)} %get-tuple-element.26), channel_id=1, source_target_pairs={{0,252},{4,0},{8,4},{12,8},{16,12},{20,16},{24,20},{28,24},{32,28}... | collective-permute-start | bytes 663560 | tf_op jit(solution)/shard_map/ppermute | solution.py:12
  53.1 4.9 %collective-permute-start.6 = (f32[1,3,8,18,128]{4,2,3,0,1:T(8,128)S(1)}, f32[1,3,8,18,128]{4,2,3,0,1:T(8,128)S(1)}, u32[]{:S(2)}, u32[]{:S(2)}) collective-permute-start(f32[1,3,8,18,128]{4,2,3,0,1:T(8,128)S(1)} %get-tuple-element.23), channel_id=1, source_target_pairs={{0,32},{4,36},{8,40},{12,44},{16,48},{20,52},{24,56},{28,60},{32,6... | collective-permute-start | bytes 663560 | tf_op jit(solution)/shard_map/ppermute | solution.py:12
  53.2 10.9 %collective-permute-start.7 = (f32[1,3,8,18,128]{4,2,3,0,1:T(8,128)S(1)}, f32[1,3,8,18,128]{4,2,3,0,1:T(8,128)S(1)}, u32[]{:S(2)}, u32[]{:S(2)}) collective-permute-start(f32[1,3,8,18,128]{4,2,3,0,1:T(8,128)S(1)} %get-tuple-element.24), channel_id=1, source_target_pairs={{0,224},{4,228},{8,232},{12,236},{16,240},{20,244},{24,248},{28,25... | collective-permute-start | bytes 663560 | tf_op jit(solution)/shard_map/ppermute | solution.py:12
  65.7 9.3 %collective-permute-start.8 = (f32[1,8,3,18,128]{4,2,3,0,1:T(4,128)S(1)}, f32[1,8,3,18,128]{4,2,3,0,1:T(4,128)S(1)}, u32[]{:S(2)}, u32[]{:S(2)}) collective-permute-start(f32[1,8,3,18,128]{4,2,3,0,1:T(4,128)S(1)} %get-tuple-element.21), channel_id=1, source_target_pairs={{0,4},{4,8},{8,12},{12,16},{16,20},{20,24},{24,28},{28,32},{32,36}... | collective-permute-start | bytes 663560 | tf_op jit(solution)/shard_map/ppermute | solution.py:12
  70.0 20.3 %collective-permute-start.9 = (f32[1,8,3,18,128]{4,2,3,0,1:T(4,128)S(1)}, f32[1,8,3,18,128]{4,2,3,0,1:T(4,128)S(1)}, u32[]{:S(2)}, u32[]{:S(2)}) collective-permute-start(f32[1,8,3,18,128]{4,2,3,0,1:T(4,128)S(1)} %get-tuple-element.22), channel_id=1, source_target_pairs={{0,252},{4,0},{8,4},{12,8},{16,12},{20,16},{24,20},{28,24},{32,28}... | collective-permute-start | bytes 663560 | tf_op jit(solution)/shard_map/ppermute | solution.py:12
  93.6 4.9 %collective-permute-start.10 = (f32[1,3,8,18,128]{4,2,3,0,1:T(8,128)S(1)}, f32[1,3,8,18,128]{4,2,3,0,1:T(8,128)S(1)}, u32[]{:S(2)}, u32[]{:S(2)}) collective-permute-start(f32[1,3,8,18,128]{4,2,3,0,1:T(8,128)S(1)} %get-tuple-element.19), channel_id=1, source_target_pairs={{0,32},{4,36},{8,40},{12,44},{16,48},{20,52},{24,56},{28,60},{32,6... | collective-permute-start | bytes 663560 | tf_op jit(solution)/shard_map/ppermute | solution.py:12
  93.7 11.0 %collective-permute-start.11 = (f32[1,3,8,18,128]{4,2,3,0,1:T(8,128)S(1)}, f32[1,3,8,18,128]{4,2,3,0,1:T(8,128)S(1)}, u32[]{:S(2)}, u32[]{:S(2)}) collective-permute-start(f32[1,3,8,18,128]{4,2,3,0,1:T(8,128)S(1)} %get-tuple-element.20), channel_id=1, source_target_pairs={{0,224},{4,228},{8,232},{12,236},{16,240},{20,244},{24,248},{28,25... | collective-permute-start | bytes 663560 | tf_op jit(solution)/shard_map/ppermute | solution.py:12
  106.4 7.1 %collective-permute-start.12 = (f32[1,8,3,18,128]{4,2,3,0,1:T(4,128)S(1)}, f32[1,8,3,18,128]{4,2,3,0,1:T(4,128)S(1)}, u32[]{:S(2)}, u32[]{:S(2)}) collective-permute-start(f32[1,8,3,18,128]{4,2,3,0,1:T(4,128)S(1)} %get-tuple-element.17), channel_id=1, source_target_pairs={{0,4},{4,8},{8,12},{12,16},{16,20},{20,24},{24,28},{28,32},{32,36}... | collective-permute-start | bytes 663560 | tf_op jit(solution)/shard_map/ppermute | solution.py:12
  108.9 18.3 %collective-permute-start.13 = (f32[1,8,3,18,128]{4,2,3,0,1:T(4,128)S(1)}, f32[1,8,3,18,128]{4,2,3,0,1:T(4,128)S(1)}, u32[]{:S(2)}, u32[]{:S(2)}) collective-permute-start(f32[1,8,3,18,128]{4,2,3,0,1:T(4,128)S(1)} %get-tuple-element.18), channel_id=1, source_target_pairs={{0,252},{4,0},{8,4},{12,8},{16,12},{20,16},{24,20},{28,24},{32,28}... | collective-permute-start | bytes 663560 | tf_op jit(solution)/shard_map/ppermute | solution.py:12
  130.9 4.4 %copy-start.1 = (f32[1,2,8,72,72]{4,3,2,1,0:T(8,128)S(1)}, f32[1,2,8,72,72]{4,3,2,1,0:T(8,128)}, u32[]{:S(2)}) copy-start(f32[1,2,8,72,72]{4,3,2,1,0:T(8,128)} %param.8) | copy-start | bytes 995332
  131.8 18.8 %all-to-all-start = ((f32[1,8,8,18,128]{4,2,3,0,1:T(8,128)}), f32[1,8,8,18,128]{4,2,3,0,1:T(8,128)S(1)}, u32[]{:S(2)}, u32[]{:S(2)}) async-start(f32[1,8,8,18,128]{4,2,3,0,1:T(8,128)} %broadcast_select_fusion), calls=%async_computation | async-start | bytes 1179648 | tf_op jit(solution)/shard_map/all_to_all | solution.py:96
where the time goes:
time: 165 us
  waiting for transfers between devices  88.5 us (54%)
  starting transfers between devices  38.7 us (23%)
  other arithmetic  17.3 us (10%)
  blocking collectives  12.3 us (7%)
  local copies, waits for them, and re-layouts  5.39 us (3%)
  between operations  1.72 us (1%)
    ppermute x14, waiting for transfers between devices, passed_along(): return lax.ppermute(value, axis, pairs)  73.6 us
    ppermute x14, starting transfers between devices, passed_along(): return lax.ppermute(value, axis, pairs)  35.2 us
    all_to_all x1, waiting for transfers between devices, on_device(): lax.all_to_all(advected, 'lev', split_axis=1, concat_axis=3, tiled=True)  14.9 us
    all_to_all x1, blocking collectives, on_device(): lax.all_to_all(mixed, 'lev', split_axis=3, concat_axis=1, tiled=True)  12.3 us
    select_n x6, other arithmetic, ppm_update(): fluxes = jnp.where(courant >= 0.0, upward, downward)  9.72 us
    all_to_all x1, starting transfers between devices, on_device(): lax.all_to_all(advected, 'lev', split_axis=1, concat_axis=3, tiled=True)  3.48 us
  transfers between devices with their start and end apart: 15, of which 12 were waited for; matrix products, arithmetic and copies ran while one was open for 3% of the time, Pallas kernels for 0%

commit v1 on v0

v1 whole, which is shorter than its diff:
```python
import jax
import jax.numpy as jnp
from jax import lax
from jax.experimental import pallas as pl
from jax.experimental.pallas import tpu as pltpu
from jax.sharding import PartitionSpec as P

MESH = pl.DeviceIdType.MESH
SUBSTEPS = 3
LEV = 18
CHUNKS = ((0, 8), (8, 4), (12, 6))
NCH = len(CHUNKS)


def swap_blocks(rows):
    lane = lax.broadcasted_iota(jnp.int32, (8, 128), 1)
    for m in (4, 2, 1):
        keep = (lane & (16 * m)) == 0
        fresh = list(rows)
        for k in range(8):
            if not k & m:
                a, b = rows[k], rows[k + m]
                fresh[k] = jnp.where(keep, a, pltpu.roll(b, 16 * m, 1))
                fresh[k + m] = jnp.where(keep, pltpu.roll(a, 128 - 16 * m, 1), b)
        rows = fresh
    return rows


def coefficients(c):
    up = c >= 0.0
    half = 0.5 * c * c
    b = half * (1.0 - jnp.abs(c) * (2.0 / 3.0))
    b = jnp.where(up, b, -b)
    signed = jnp.where(up, half, -half)
    return (c - signed - 3.0 * b) * (1.0 / 12.0), (signed - 3.0 * b) * (1.0 / 12.0), 6.0 * b


def face_value(q0, q1, q2, q3):
    return 7.0 * (q1 + q2) - (q0 + q3)


def face_flux(mid, below, above, q_below, q_above, ka, ku, kq):
    up = kq >= 0.0
    return ka * mid + ku * jnp.where(up, below, above) + kq * jnp.where(up, q_below, q_above)


def kernel(
    x_ref, c1_ref, c2_ref, w_ref, f_ref, o_ref,
    staged, send, recv, c_tmp, c_send, c_recv, raw, flags,
    fa, fb, halo_low, halo_high, edge_send, edge_recv,
    k1, k2, mix_send, mix_recv, columns, matrix, mixed,
    a_ssem, a_rsem, c_ssem, c_rsem, h_ssem, h_rsem, e_ssem, e_rsem, m_ssem, m_rsem, d_ssem, d_rsem, l_sem,
):
    t = lax.axis_index("tile")
    l = lax.axis_index("lev")
    ring = t // 8
    yc = t % 8
    hi = ring // 4
    x = ring % 4
    z = hi * 4 + l
    group = (l + 2) % 4
    eighth = (((z + 6) % 8) // 4) * 4 + x

    def at(zz, xx):
        return {"tile": ((zz // 4) * 4 + xx) * 8 + yc, "lev": zz % 4}

    low = {"tile": ring * 8 + (yc + 7) % 8, "lev": l}
    high = {"tile": ring * 8 + (yc + 1) % 8, "lev": l}

    barrier = pltpu.get_barrier_semaphore()

    def greet(o, carry):
        pl.semaphore_signal(barrier, inc=1, device_id=at((z + o // 4) % 8, (x + o % 4) % 4), device_id_type=MESH)
        return carry

    lax.fori_loop(1, 32, greet, 0)
    pl.semaphore_signal(barrier, inc=1, device_id=low, device_id_type=MESH)
    pl.semaphore_signal(barrier, inc=1, device_id=high, device_id_type=MESH)

    flip_i = f_ref[0, 0]
    flip_j = f_ref[0, 1]
    c_tmp[...] = jnp.zeros((128, 128), jnp.float32)
    for i in range(8):
        c_tmp[8 * i:8 * i + 8, 0:LEV] = c1_ref[0, i]
        c_tmp[64 + 8 * i:72 + 8 * i, 0:LEV] = c2_ref[0, i]
    turned = c_tmp[...].T
    c_send[...] = turned[0:24]
    c_send[18:19, :] = jnp.full((1, 128), flip_i, jnp.int32).astype(jnp.float32)
    c_send[19:20, :] = jnp.full((1, 128), flip_j, jnp.int32).astype(jnp.float32)

    def stage(i, carry):
        i2 = i + flip_i * (7 - 2 * i)
        for j in range(8):
            j2 = j + flip_j * (7 - 2 * j)
            staged[pl.ds(i * 8 + j, LEV, stride=64), :] = x_ref[0, i2, j2]
        return carry

    lax.fori_loop(0, 8, stage, 0)

    def pack(lev, carry):
        rows = [staged[pl.ds(pl.multiple_of(lev * 64 + 8 * i, 8), 8), :] for i in range(8)]
        rows = swap_blocks(rows)
        for d in range(8):
            send[d, lev] = rows[d]
        return carry

    lax.fori_loop(0, LEV, pack, 0)

    pl.semaphore_wait(barrier, 33)

    def target(d):
        return at((l + 2 + 4 * (d // 4)) % 8, d % 4)

    def c_copy(d, slot):
        return pltpu.make_async_remote_copy(
            src_ref=c_send, dst_ref=c_recv.at[pl.ds(slot * 24, 24)],
            send_sem=c_ssem.at[d], recv_sem=c_rsem.at[slot], device_id=target(d), device_id_type=MESH)

    def a_copy(d, slot, ch):
        first, count = CHUNKS[ch]
        return pltpu.make_async_remote_copy(
            src_ref=send.at[d, pl.ds(first, count)], dst_ref=recv.at[slot, pl.ds(first, count)],
            send_sem=a_ssem.at[d, ch], recv_sem=a_rsem.at[slot, ch], device_id=target(d), device_id_type=MESH)

    for d in range(8):
        c_copy(d, ring).start()
    for ch in range(NCH):
        for d in range(8):
            a_copy(d, ring, ch).start()

    def prepare(cell, carry):
        s, j = cell // 8, cell % 8
        for part in range(4):
            w = w_ref[0, s, j, 18 * part:18 * part + 18, :]
            same = lax.broadcasted_iota(jnp.int32, (18, 72), 1) == lax.broadcasted_iota(jnp.int32, (18, 72), 0) + 18 * part
            total = jnp.sum(w, axis=-1, keepdims=True)
            matrix[cell, 24 * part:24 * part + 18, :] = 0.4 * (w / total) + jnp.where(same, 0.6, 0.0)
        return carry

    lax.fori_loop(0, 16, prepare, 0)

    for slot in range(8):
        c_copy(slot, slot).wait_recv()
    spread = (
        lax.broadcasted_iota(jnp.int32, (24, 128), 0) % 8 == lax.broadcasted_iota(jnp.int32, (24, 128), 1) // 16
    ).astype(jnp.float32).astype(jnp.bfloat16)

    def spread_level(lev):
        v = c_recv[pl.ds(lev, 8, stride=24), :]
        p0 = v.astype(jnp.bfloat16).astype(jnp.float32)
        p1 = (v - p0).astype(jnp.bfloat16).astype(jnp.float32)
        p2 = v - p0 - p1
        parts = jnp.concatenate([p0, p1, p2], axis=0).astype(jnp.bfloat16)
        return lax.dot_general(parts, spread, (((0,), (0,)), ((), ())), preferred_element_type=jnp.float32)

    def courant(lev, carry):
        wide = spread_level(lev)
        for i in range(8):
            for n, value in enumerate(coefficients(wide[8 * i:8 * i + 8])):
                k1[n, lev, 8 * i:8 * i + 8, :] = value
            raw[pl.ds(i, 8, stride=8), :] = wide[64 + 8 * i:72 + 8 * i]
        for j in range(8):
            for n, value in enumerate(coefficients(raw[8 * j:8 * j + 8, :])):
                k2[n, lev, 8 * j + 8:8 * j + 16, :] = value
        edge_send[lev] = raw[56:64, :]
        return carry

    lax.fori_loop(0, LEV, courant, 0)
    for n in range(2):
        flags[n] = spread_level(18 + n)[0:8]

    edge = pltpu.make_async_remote_copy(
        src_ref=edge_send, dst_ref=edge_recv, send_sem=e_ssem, recv_sem=e_rsem, device_id=high, device_id_type=MESH)
    edge.start()

    roll_low = jnp.where(yc == 0, 16, 0)
    roll_high = jnp.where(yc == 7, 112, 0)

    def unpack(ch):
        first, count = CHUNKS[ch]
        for slot in range(8):
            a_copy(slot, slot, ch).wait_recv()

        def one(lev, carry):
            rows = swap_blocks([recv[slot, lev] for slot in range(8)])
            for i in range(8):
                fa[lev, 8 * i:8 * i + 8, :] = rows[i]
            return carry

        lax.fori_loop(first, first + count, one, 0)

    def sweep_first(step, ch):
        first, count = CHUNKS[ch]

        def one(lev, carry):
            q = [fa[lev, 8 * i:8 * i + 8, :] for i in range(8)]
            e = [pltpu.roll(q[7], 16, 1)] + q + [pltpu.roll(q[0], 112, 1), pltpu.roll(q[1], 112, 1)]
            a = [face_value(*e[i:i + 4]) for i in range(8)]
            a = [pltpu.roll(a[7], 16, 1)] + a + [pltpu.roll(a[0], 112, 1)]
            flux = []
            for i in range(8):
                k = [k1[n, lev, 8 * i:8 * i + 8, :] for n in range(3)]
                flux.append(face_flux(a[i + 1], a[i], a[i + 2], e[i + 1], e[i + 2], *k))
            flux = [pltpu.roll(flux[7], 16, 1)] + flux
            for i in range(8):
                fb[step, lev, pl.ds(i, 8, stride=8), :] = q[i] - (flux[i + 1] - flux[i])
            return carry

        lax.fori_loop(first, first + count, one, 0)

    def halo_copies(step, ch):
        first, count = CHUNKS[ch]
        return (
            pltpu.make_async_remote_copy(
                src_ref=fb.at[step, pl.ds(first, count), pl.ds(40, 24)], dst_ref=halo_low.at[step, pl.ds(first, count)],
                send_sem=h_ssem.at[0, step, ch], recv_sem=h_rsem.at[0, step, ch], device_id=high, device_id_type=MESH),
            pltpu.make_async_remote_copy(
                src_ref=fb.at[step, pl.ds(first, count), pl.ds(0, 24)], dst_ref=halo_high.at[step, pl.ds(first, count)],
                send_sem=h_ssem.at[1, step, ch], recv_sem=h_rsem.at[1, step, ch], device_id=low, device_id_type=MESH),
        )

    def sweep_second(step, ch):
        first, count = CHUNKS[ch]
        last = step == SUBSTEPS - 1

        def one(lev, carry):
            q = [fb[step, lev, 8 * j:8 * j + 8, :] for j in range(8)]
            e = [pltpu.roll(halo_low[step, lev, 8 * j:8 * j + 8, :], roll_low, 1) for j in range(3)] + q
            e += [pltpu.roll(halo_high[step, lev, 8 * j:8 * j + 8, :], roll_high, 1) for j in range(3)]
            a = [face_value(*e[k:k + 4]) for k in range(11)]
            flux = []
            for f in range(9):
                k = [k2[n, lev, 8 * f:8 * f + 8, :] for n in range(3)]
                flux.append(face_flux(a[f + 1], a[f], a[f + 2], e[f + 2], e[f + 3], *k))
            new = [q[j] - (flux[j + 1] - flux[j]) for j in range(8)]
            if last:
                back = flags[1] > 0.5
                new = [jnp.where(back, new[7 - j], new[j]) for j in range(8)]
            for j in range(8):
                fa[lev, pl.ds(j, 8, stride=8), :] = new[j]
            return carry

        lax.fori_loop(first, first + count, one, 0)

    for ch in range(NCH):
        unpack(ch)
        sweep_first(0, ch)
        for copy in halo_copies(0, ch):
            copy.start()

    edge.wait_recv()

    def edge_level(lev, carry):
        for n, value in enumerate(coefficients(pltpu.roll(edge_recv[lev], roll_low, 1))):
            k2[n, lev, 0:8, :] = value
        return carry

    lax.fori_loop(0, LEV, edge_level, 0)

    for step in range(SUBSTEPS):
        for ch in range(NCH):
            for copy in halo_copies(step, ch):
                copy.wait_recv()
            sweep_second(step, ch)
            if step < SUBSTEPS - 1:
                sweep_first(step + 1, ch)
                for copy in halo_copies(step + 1, ch):
                    copy.start()

    def mix_pack(r, carry):
        back = flags[0] > 0.5
        for m in range(5):
            rows = []
            for k in range(8):
                lev, i = 4 * m + k // 2, 2 * r + k % 2
                if lev < LEV:
                    here = fa[lev, pl.ds(pl.multiple_of(8 * i, 8), 8), :]
                    there = fa[lev, pl.ds(pl.multiple_of(56 - 8 * i, 8), 8), :]
                    rows.append(jnp.where(back, there, here))
                else:
                    rows.append(jnp.zeros((8, 128), jnp.float32))
            rows = swap_blocks(rows)
            for k in range(8):
                mix_send[k * 4 + r, m] = rows[k]
        return carry

    lax.fori_loop(0, 4, mix_pack, 0)

    def m_copy(o):
        zd, xd = (z + o // 4) % 8, (x + o % 4) % 4
        return pltpu.make_async_remote_copy(
            src_ref=mix_send.at[((zd // 4) * 4 + xd) * 4 + zd % 4], dst_ref=mix_recv.at[group * 8 + eighth],
            send_sem=m_ssem.at[o], recv_sem=m_rsem.at[o], device_id=at(zd, xd), device_id_type=MESH)

    def m_arrival(o):
        zs, xs = (z + 8 - o // 4) % 8, (x + 4 - o % 4) % 4
        slot = ((zs + 2) % 4) * 8 + (((zs + 6) % 8) // 4) * 4 + xs
        return pltpu.make_async_remote_copy(
            src_ref=mix_send.at[0], dst_ref=mix_recv.at[slot],
            send_sem=m_ssem.at[o], recv_sem=m_rsem.at[o], device_id=at(zs, xs), device_id_type=MESH)

    def m_start(o, carry):
        m_copy(o).start()
        return carry

    lax.fori_loop(1, 32, m_start, 0)
    own = pltpu.make_async_copy(mix_send.at[ring * 4 + l], mix_recv.at[group * 8 + eighth], l_sem.at[0])
    own.start()

    def m_wait(o, carry):
        m_arrival(o).wait_recv()
        return carry

    lax.fori_loop(1, 32, m_wait, 0)
    own.wait()

    def mix_unpack(g, carry):
        for m in range(5):
            rows = swap_blocks([mix_recv[g * 8 + k, m] for k in range(8)])
            for k in range(8):
                lev, s = 4 * m + k // 2, k % 2
                if lev < LEV:
                    columns[s, pl.ds(pl.multiple_of((g * LEV + lev) * 8, 8), 8), :] = rows[k]
        return carry

    lax.fori_loop(0, 4, mix_unpack, 0)

    def d_copy(s, o):
        to = (l + o) % 4
        return pltpu.make_async_remote_copy(
            src_ref=mixed.at[s, to], dst_ref=o_ref.at[0, 2 * l + s],
            send_sem=d_ssem.at[s, o], recv_sem=d_rsem.at[s, o], device_id={"tile": t, "lev": to}, device_id_type=MESH)

    def d_arrival(s, o):
        source = (l + 4 - o) % 4
        return pltpu.make_async_remote_copy(
            src_ref=mixed.at[s, 0], dst_ref=o_ref.at[0, 2 * source + s],
            send_sem=d_ssem.at[s, o], recv_sem=d_rsem.at[s, o], device_id={"tile": t, "lev": source}, device_id_type=MESH)

    def mix_row(s):
        def one(j, carry):
            v = columns[s, pl.ds(j, 72, stride=8), :]
            v_hi = v.astype(jnp.bfloat16)
            v_lo = (v - v_hi.astype(jnp.float32)).astype(jnp.bfloat16)
            m = matrix[s * 8 + j]
            m_hi = m.astype(jnp.bfloat16)
            m_lo = (m - m_hi.astype(jnp.float32)).astype(jnp.bfloat16)
            dot = lambda a, b: jnp.dot(a, b, preferred_element_type=jnp.float32)
            out = dot(m_hi, v_hi) + (dot(m_hi, v_lo) + dot(m_lo, v_hi))
            for part in range(4):
                mixed[s, part, j] = out[24 * part:24 * part + 18]
            return carry

        lax.fori_loop(0, 8, one, 0)

    local = []
    for s in range(2):
        mix_row(s)
        for o in range(1, 4):
            d_copy(s, o).start()
        local.append(pltpu.make_async_copy(mixed.at[s, l], o_ref.at[0, 2 * l + s], l_sem.at[1 + s]))
        local[s].start()

    for d in range(8):
        c_copy(d, ring).wait_send()
        for ch in range(NCH):
            a_copy(d, ring, ch).wait_send()
    edge.wait_send()
    for step in range(SUBSTEPS):
        for ch in range(NCH):
            for copy in halo_copies(step, ch):
                copy.wait_send()

    def m_end(o, carry):
        m_copy(o).wait_send()
        return carry

    lax.fori_loop(1, 32, m_end, 0)
    for s in range(2):
        for o in range(1, 4):
            d_copy(s, o).wait_send()
            d_arrival(s, o).wait_recv()
        local[s].wait()


def solution(mesh):
    f32 = jnp.float32

    def on_device(tracers, courant_first, courant_second, weights, frame_flip):
        vmem = pl.BlockSpec(memory_space=pltpu.VMEM)
        dma = pltpu.SemaphoreType.DMA
        return pl.pallas_call(
            kernel,
            out_shape=jax.ShapeDtypeStruct(tracers.shape, f32),
            in_specs=[vmem, vmem, vmem, vmem, pl.BlockSpec(memory_space=pltpu.SMEM)],
            out_specs=vmem,
            scratch_shapes=[
                pltpu.VMEM((LEV * 64, 128), f32),
                pltpu.VMEM((8, LEV, 8, 128), f32),
                pltpu.VMEM((8, LEV, 8, 128), f32),
                pltpu.VMEM((128, 128), f32),
                pltpu.VMEM((24, 128), f32),
                pltpu.VMEM((192, 128), f32),
                pltpu.VMEM((64, 128), f32),
                pltpu.VMEM((2, 8, 128), f32),
                pltpu.VMEM((LEV, 64, 128), f32),
                pltpu.VMEM((SUBSTEPS, LEV, 64, 128), f32),
                pltpu.VMEM((SUBSTEPS, LEV, 24, 128), f32),
                pltpu.VMEM((SUBSTEPS, LEV, 24, 128), f32),
                pltpu.VMEM((LEV, 8, 128), f32),
                pltpu.VMEM((LEV, 8, 128), f32),
                pltpu.VMEM((3, LEV, 64, 128), f32),
                pltpu.VMEM((3, LEV, 72, 128), f32),
                pltpu.VMEM((32, 5, 8, 128), f32),
                pltpu.VMEM((32, 5, 8, 128), f32),
                pltpu.VMEM((2, 72 * 8, 128), f32),
                pltpu.VMEM((16, 96, 72), f32),
                pltpu.VMEM((2, 4, 8, LEV, 128), f32),
                dma((8, NCH)), dma((8, NCH)),
                dma((8,)), dma((8,)),
                dma((2, SUBSTEPS, NCH)), dma((2, SUBSTEPS, NCH)),
                dma, dma,
                dma((32,)), dma((32,)),
                dma((2, 4)), dma((2, 4)),
                dma((3,)),
            ],
            compiler_params=pltpu.CompilerParams(collective_id=0, has_side_effects=True),
        )(tracers, courant_first, courant_second, weights, frame_flip)

    return jax.shard_map(
        on_device,
        mesh=mesh,
        in_specs=(
            P("tile", None, None, "lev", None),
            P("tile", None, None, "lev"),
            P("tile", None, None, "lev"),
            P("tile", "lev", None, None, None),
            P("tile", None),
        ),
        out_specs=P("tile", None, None, "lev", None),
        check_vma=False,
    )
```

time: 165 us -> 92.5 us (0.56)
  the two profiles are of different devices: /device:TPU:31 before, /device:TPU:41 now
where the time goes in v1:
time: 92.5 us; the launch traced here: 92.4 us
  Pallas kernels  88.2 us (95%)
  local copies, waits for them, and re-layouts  4.12 us (4%)
    pallas_call x1, Pallas kernels, on_device(): pl.pallas_call(kernel, out_shape=jax.ShapeDtypeStruct(tracers.shape, f32)...  88.2 us
    unnamed x1, local copies, waits for them, and re-layouts  2.07 us
    pallas_call x1, local copies, waits for them, and re-layouts, on_device(): pl.pallas_call(kernel, out_shape=jax.ShapeDtypeStruct(tracers.shape, f32)...  2.05 us

profile of v1, /device:TPU:41, one launch (start us, length us, event | category | flops | bytes accessed | tf_op | source)
XLA Modules:
  0.0 92.4 jit_solution(17095340569482820772)
XLA Ops:
  0.0 2.1 %copy.6.x_ref = f32[1,8,8,18,128]{4,3,2,1,0:T(8,128)} copy(f32[1,8,8,18,128]{4,2,3,1,0:T(8,128)} %param.5) | data formatting | bytes 1179648 | tf_op args[0]
  2.1 88.2 %shard_map.55 = f32[1,8,8,18,128]{4,3,2,1,0:T(8,128)} custom-call(f32[1,8,8,18,128]{4,3,2,1,0:T(8,128)} %copy.6.x_ref, f32[1,8,8,18]{3,2,1,0:T(8,128)} %c1_ref.1, f32[1,8,8,18]{3,2,1,0:T(8,128)} %c2_ref.1, f32[1,2,8,72,72]{4,3,2,1,0:T(8,128)} %w_ref.1, s32[1,2]{1,0:T(1,128)} %f_ref.1), custom_call_target="tpu_custom_call" | custom-call | tf_op jit(solution)/shard_map/pallas_call | solution.py:392
  90.3 2.1 %copy.7 = f32[1,8,8,18,128]{4,2,3,1,0:T(8,128)} copy(f32[1,8,8,18,128]{4,3,2,1,0:T(8,128)} %shard_map.55) | data formatting | bytes 1179648 | tf_op jit(solution)/shard_map/pallas_call | solution.py:392

commit v2 on v1

--- a/solution.py
+++ b/solution.py
@@ -10,6 +10,7 @@
 LEV = 18
 CHUNKS = ((0, 8), (8, 4), (12, 6))
 NCH = len(CHUNKS)
+UNROLL = 2
 
 
 def swap_blocks(rows):
@@ -26,6 +27,13 @@
     return rows
 
 
+def reverse_rows(v):
+    row = lax.broadcasted_iota(jnp.int32, (8, 128), 0)
+    v = pltpu.roll(v, 4, 0)
+    v = jnp.where((row & 2) == 0, pltpu.roll(v, 6, 0), pltpu.roll(v, 2, 0))
+    return jnp.where((row & 1) == 0, pltpu.roll(v, 7, 0), pltpu.roll(v, 1, 0))
+
+
 def coefficients(c):
     up = c >= 0.0
     half = 0.5 * c * c
@@ -46,10 +54,10 @@
 
 def kernel(
     x_ref, c1_ref, c2_ref, w_ref, f_ref, o_ref,
-    staged, send, recv, c_tmp, c_send, c_recv, raw, flags,
+    x_vmem, w_vmem, send, recv, c_tmp, c_send, c_recv, raw, flags,
     fa, fb, halo_low, halo_high, edge_send, edge_recv,
     k1, k2, mix_send, mix_recv, columns, matrix, mixed,
-    a_ssem, a_rsem, c_ssem, c_rsem, h_ssem, h_rsem, e_ssem, e_rsem, m_ssem, m_rsem, d_ssem, d_rsem, l_sem,
+    a_ssem, a_rsem, c_ssem, c_rsem, h_ssem, h_rsem, e_ssem, e_rsem, m_ssem, m_rsem, d_ssem, d_rsem, l_sem, i_sem,
 ):
     t = lax.axis_index("tile")
     l = lax.axis_index("lev")
@@ -68,14 +76,14 @@
     high = {"tile": ring * 8 + (yc + 1) % 8, "lev": l}
 
     barrier = pltpu.get_barrier_semaphore()
-
-    def greet(o, carry):
-        pl.semaphore_signal(barrier, inc=1, device_id=at((z + o // 4) % 8, (x + o % 4) % 4), device_id_type=MESH)
-        return carry
-
-    lax.fori_loop(1, 32, greet, 0)
-    pl.semaphore_signal(barrier, inc=1, device_id=low, device_id_type=MESH)
-    pl.semaphore_signal(barrier, inc=1, device_id=high, device_id_type=MESH)
+    greeted = [at((z + dz) % 8, (x + dx) % 4) for dz in (2, 6) for dx in range(4)]
+    greeted += [at((z + 1) % 8, x), at((z + 7) % 8, x), low, high]
+    for device in greeted:
+        pl.semaphore_signal(barrier, inc=1, device_id=device, device_id_type=MESH)
+    x_load = pltpu.make_async_copy(x_ref.at[0], x_vmem, i_sem.at[0])
+    w_load = pltpu.make_async_copy(w_ref.at[0], w_vmem, i_sem.at[1])
+    x_load.start()
+    w_load.start()
 
     flip_i = f_ref[0, 0]
     flip_j = f_ref[0, 1]
@@ -88,25 +96,19 @@
     c_send[18:19, :] = jnp.full((1, 128), flip_i, jnp.int32).astype(jnp.float32)
     c_send[19:20, :] = jnp.full((1, 128), flip_j, jnp.int32).astype(jnp.float32)
 
-    def stage(i, carry):
-        i2 = i + flip_i * (7 - 2 * i)
-        for j in range(8):
-            j2 = j + flip_j * (7 - 2 * j)
-            staged[pl.ds(i * 8 + j, LEV, stride=64), :] = x_ref[0, i2, j2]
-        return carry
-
-    lax.fori_loop(0, 8, stage, 0)
+    x_load.wait()
+    turn = jnp.full((8, 128), flip_j, jnp.int32) == 1
 
     def pack(lev, carry):
-        rows = [staged[pl.ds(pl.multiple_of(lev * 64 + 8 * i, 8), 8), :] for i in range(8)]
-        rows = swap_blocks(rows)
+        rows = [x_vmem[i + flip_i * (7 - 2 * i), lev] for i in range(8)]
+        rows = swap_blocks([jnp.where(turn, reverse_rows(v), v) for v in rows])
         for d in range(8):
             send[d, lev] = rows[d]
         return carry
 
     lax.fori_loop(0, LEV, pack, 0)
 
-    pl.semaphore_wait(barrier, 33)
+    pl.semaphore_wait(barrier, len(greeted))
 
     def target(d):
         return at((l + 2 + 4 * (d // 4)) % 8, d % 4)
@@ -128,13 +130,15 @@
         for d in range(8):
             a_copy(d, ring, ch).start()
 
+    w_load.wait()
+    diagonal = jnp.where(
+        lax.broadcasted_iota(jnp.int32, (72, 72), 0) == lax.broadcasted_iota(jnp.int32, (72, 72), 1), 0.6, 0.0)
+
     def prepare(cell, carry):
         s, j = cell // 8, cell % 8
-        for part in range(4):
-            w = w_ref[0, s, j, 18 * part:18 * part + 18, :]
-            same = lax.broadcasted_iota(jnp.int32, (18, 72), 1) == lax.broadcasted_iota(jnp.int32, (18, 72), 0) + 18 * part
-            total = jnp.sum(w, axis=-1, keepdims=True)
-            matrix[cell, 24 * part:24 * part + 18, :] = 0.4 * (w / total) + jnp.where(same, 0.6, 0.0)
+        w = w_vmem[s, j]
+        total = jnp.sum(w, axis=-1, keepdims=True)
+        matrix[cell] = 0.4 * (w / total) + diagonal
         return carry
 
     lax.fori_loop(0, 16, prepare, 0)
@@ -192,7 +196,7 @@
     def sweep_first(step, ch):
         first, count = CHUNKS[ch]
 
-        def one(lev, carry):
+        def level(lev):
             q = [fa[lev, 8 * i:8 * i + 8, :] for i in range(8)]
             e = [pltpu.roll(q[7], 16, 1)] + q + [pltpu.roll(q[0], 112, 1), pltpu.roll(q[1], 112, 1)]
             a = [face_value(*e[i:i + 4]) for i in range(8)]
@@ -202,11 +206,17 @@
                 k = [k1[n, lev, 8 * i:8 * i + 8, :] for n in range(3)]
                 flux.append(face_flux(a[i + 1], a[i], a[i + 2], e[i + 1], e[i + 2], *k))
             flux = [pltpu.roll(flux[7], 16, 1)] + flux
-            for i in range(8):
-                fb[step, lev, pl.ds(i, 8, stride=8), :] = q[i] - (flux[i + 1] - flux[i])
+            return [q[i] - (flux[i + 1] - flux[i]) for i in range(8)]
+
+        def some(n, carry):
+            levels = [first + n * UNROLL + k for k in range(UNROLL)]
+            new = [level(lev) for lev in levels]
+            for lev, rows in zip(levels, new):
+                for i in range(8):
+                    fb[step, lev, pl.ds(i, 8, stride=8), :] = rows[i]
             return carry
 
-        lax.fori_loop(first, first + count, one, 0)
+        lax.fori_loop(0, count // UNROLL, some, 0)
 
     def halo_copies(step, ch):
         first, count = CHUNKS[ch]
@@ -223,7 +233,7 @@
         first, count = CHUNKS[ch]
         last = step == SUBSTEPS - 1
 
-        def one(lev, carry):
+        def level(lev):
             q = [fb[step, lev, 8 * j:8 * j + 8, :] for j in range(8)]
             e = [pltpu.roll(halo_low[step, lev, 8 * j:8 * j + 8, :], roll_low, 1) for j in range(3)] + q
             e += [pltpu.roll(halo_high[step, lev, 8 * j:8 * j + 8, :], roll_high, 1) for j in range(3)]
@@ -236,11 +246,17 @@
             if last:
                 back = flags[1] > 0.5
                 new = [jnp.where(back, new[7 - j], new[j]) for j in range(8)]
-            for j in range(8):
-                fa[lev, pl.ds(j, 8, stride=8), :] = new[j]
+            return new
+
+        def some(n, carry):
+            levels = [first + n * UNROLL + k for k in range(UNROLL)]
+            new = [level(lev) for lev in levels]
+            for lev, rows in zip(levels, new):
+                for j in range(8):
+                    fa[lev, pl.ds(j, 8, stride=8), :] = rows[j]
             return carry
 
-        lax.fori_loop(first, first + count, one, 0)
+        lax.fori_loop(0, count // UNROLL, some, 0)
 
     for ch in range(NCH):
         unpack(ch)
@@ -328,13 +344,13 @@
     def d_copy(s, o):
         to = (l + o) % 4
         return pltpu.make_async_remote_copy(
-            src_ref=mixed.at[s, to], dst_ref=o_ref.at[0, 2 * l + s],
+            src_ref=mixed.at[s, pl.ds(to * 144, 144)], dst_ref=o_ref.at[0, 2 * l + s],
             send_sem=d_ssem.at[s, o], recv_sem=d_rsem.at[s, o], device_id={"tile": t, "lev": to}, device_id_type=MESH)
 
     def d_arrival(s, o):
         source = (l + 4 - o) % 4
         return pltpu.make_async_remote_copy(
-            src_ref=mixed.at[s, 0], dst_ref=o_ref.at[0, 2 * source + s],
+            src_ref=mixed.at[s, pl.ds(0, 144)], dst_ref=o_ref.at[0, 2 * source + s],
             send_sem=d_ssem.at[s, o], recv_sem=d_rsem.at[s, o], device_id={"tile": t, "lev": source}, device_id_type=MESH)
 
     def mix_row(s):
@@ -347,8 +363,7 @@
             m_lo = (m - m_hi.astype(jnp.float32)).astype(jnp.bfloat16)
             dot = lambda a, b: jnp.dot(a, b, preferred_element_type=jnp.float32)
             out = dot(m_hi, v_hi) + (dot(m_hi, v_lo) + dot(m_lo, v_hi))
-            for part in range(4):
-                mixed[s, part, j] = out[24 * part:24 * part + 18]
+            mixed[s, pl.ds(j, 72, stride=8), :] = out
             return carry
 
         lax.fori_loop(0, 8, one, 0)
@@ -358,7 +373,7 @@
         mix_row(s)
         for o in range(1, 4):
             d_copy(s, o).start()
-        local.append(pltpu.make_async_copy(mixed.at[s, l], o_ref.at[0, 2 * l + s], l_sem.at[1 + s]))
+        local.append(pltpu.make_async_copy(mixed.at[s, pl.ds(l * 144, 144)], o_ref.at[0, 2 * l + s], l_sem.at[1 + s]))
         local[s].start()
 
     for d in range(8):
@@ -388,14 +403,17 @@
 
     def on_device(tracers, courant_first, courant_second, weights, frame_flip):
         vmem = pl.BlockSpec(memory_space=pltpu.VMEM)
+        hbm = pl.BlockSpec(memory_space=pl.ANY)
         dma = pltpu.SemaphoreType.DMA
-        return pl.pallas_call(
+        rows = jnp.transpose(tracers, (0, 1, 3, 2, 4)).reshape(1, 8, LEV, 8, 128)
+        out = pl.pallas_call(
             kernel,
-            out_shape=jax.ShapeDtypeStruct(tracers.shape, f32),
-            in_specs=[vmem, vmem, vmem, vmem, pl.BlockSpec(memory_space=pltpu.SMEM)],
+            out_shape=jax.ShapeDtypeStruct((1, 8, LEV * 8, 128), f32),
+            in_specs=[hbm, vmem, vmem, hbm, pl.BlockSpec(memory_space=pltpu.SMEM)],
             out_specs=vmem,
             scratch_shapes=[
-                pltpu.VMEM((LEV * 64, 128), f32),
+                pltpu.VMEM((8, LEV, 8, 128), f32),
+                pltpu.VMEM((2, 8, 72, 72), f32),
                 pltpu.VMEM((8, LEV, 8, 128), f32),
                 pltpu.VMEM((8, LEV, 8, 128), f32),
                 pltpu.VMEM((128, 128), f32),
@@ -414,8 +432,8 @@
                 pltpu.VMEM((32, 5, 8, 128), f32),
                 pltpu.VMEM((32, 5, 8, 128), f32),
                 pltpu.VMEM((2, 72 * 8, 128), f32),
-                pltpu.VMEM((16, 96, 72), f32),
-                pltpu.VMEM((2, 4, 8, LEV, 128), f32),
+                pltpu.VMEM((16, 72, 72), f32),
+                pltpu.VMEM((2, 72 * 8, 128), f32),
                 dma((8, NCH)), dma((8, NCH)),
                 dma((8,)), dma((8,)),
                 dma((2, SUBSTEPS, NCH)), dma((2, SUBSTEPS, NCH)),
@@ -423,9 +441,11 @@
                 dma((32,)), dma((32,)),
                 dma((2, 4)), dma((2, 4)),
                 dma((3,)),
+                dma((2,)),
             ],
             compiler_params=pltpu.CompilerParams(collective_id=0, has_side_effects=True),
-        )(tracers, courant_first, courant_second, weights, frame_flip)
+        )(rows, courant_first, courant_second, weights, frame_flip)
+        return jnp.transpose(out.reshape(1, 8, LEV, 8, 128), (0, 1, 3, 2, 4))
 
     return jax.shard_map(
         on_device,

time: 92.5 us -> 83.5 us (0.903)
  Pallas kernels: 88.2 us -> 81.4 us
  local copies, waits for them, and re-layouts: 4.12 us -> 1.92 us
    pallas_call x1, Pallas kernels: 88.2 us -> 81.4 us  [on_device(): pl.pallas_call(kernel, out_shape=jax.ShapeDtypeStruct((1, 8, LEV * 8, 128...]
    pallas_call x1 -> x0, local copies, waits for them, and re-layouts: 2.05 us -> none  [on_device(): pl.pallas_call(kernel, out_shape=jax.ShapeDtypeStruct(tracers.shape, f32)...]
where the time goes in v2:
time: 83.5 us; the launch traced here: 83.3 us
  Pallas kernels  81.4 us (97%)
  local copies, waits for them, and re-layouts  1.92 us (2%)
    pallas_call x1, Pallas kernels, on_device(): pl.pallas_call(kernel, out_shape=jax.ShapeDtypeStruct((1, 8, LEV * 8, 128...  81.4 us
    unnamed x1, local copies, waits for them, and re-layouts  1.92 us

profile of v2, /device:TPU:41, one launch (start us, length us, event | category | flops | bytes accessed | tf_op | source)
XLA Modules:
  0.0 83.3 jit_solution(18032770020404511284)
XLA Ops:
  0.0 81.4 %shard_map.55 = f32[1,8,144,128]{3,2,1,0:T(8,128)} custom-call(f32[1,8,18,8,128]{4,3,2,1,0:T(8,128)} %bitcast.5, f32[1,8,8,18]{3,2,1,0:T(8,128)} %c1_ref.1, f32[1,8,8,18]{3,2,1,0:T(8,128)} %c2_ref.1, f32[1,2,8,72,72]{4,3,2,1,0:T(8,128)} %w_ref.1, s32[1,2]{1,0:T(1,128)} %f_ref.1), custom_call_target="tpu_custom_call" | custom-call | tf_op jit(solution)/shard_map/pallas_call | solution.py:409
  81.4 1.9 %copy.7 = f32[1,8,8,18,128]{4,2,3,1,0:T(8,128)} copy(f32[1,8,8,18,128]{4,2,3,1,0:T(8,128)} %bitcast.4) | data formatting | bytes 1179648

commit v3 on v2

v3 whole, which is shorter than its diff:
```python
import jax
import jax.numpy as jnp
from jax import lax
from jax.experimental import pallas as pl
from jax.experimental.pallas import tpu as pltpu
from jax.sharding import PartitionSpec as P

MESH = pl.DeviceIdType.MESH
SUBSTEPS = 3
LEV = 18
CHUNKS = ((0, 8), (8, 4), (12, 6))
NCH = len(CHUNKS)
GROUPS = tuple(tuple(range(first // 4, (first + count + 3) // 4)) for first, count in CHUNKS)
UNROLL = 2


def turn_blocks(rows):
    return [pltpu.roll(v, 16 * k, 1) if k else v for k, v in enumerate(rows)]


def pick_blocks(rows):
    block = lax.broadcasted_iota(jnp.int32, (8, 128), 1) // 16
    rows = [rows[(8 - b) % 8] for b in range(8)]
    for m in (1, 2, 4):
        other = (block & m) != 0
        rows = [jnp.where(other, rows[(b + 8 - m) % 8], rows[b]) for b in range(8)]
    return rows


def turn_back(rows):
    return [pltpu.roll(v, 128 - 16 * b, 1) if b else v for b, v in enumerate(rows)]


def coefficients(c):
    up = c >= 0.0
    half = 0.5 * c * c
    b = half * (1.0 - jnp.abs(c) * (2.0 / 3.0))
    b = jnp.where(up, b, -b)
    signed = jnp.where(up, half, -half)
    return (c - signed - 3.0 * b) * (1.0 / 12.0), (signed - 3.0 * b) * (1.0 / 12.0), 6.0 * b


def face_value(q0, q1, q2, q3):
    return 7.0 * (q1 + q2) - (q0 + q3)


def face_flux(mid, below, above, q_below, q_above, ka, ku, kq):
    up = kq >= 0.0
    return ka * mid + ku * jnp.where(up, below, above) + kq * jnp.where(up, q_below, q_above)


def kernel(
    x_ref, c1_ref, c2_ref, w_ref, f_ref, o_ref,
    x_vmem, w_vmem, send, recv, c_tmp, c_send, c_recv, raw, flags,
    fa, fb, halo_low, halo_high, edge_send, edge_recv,
    k1, k2, mix_send, mix_recv, columns, matrix, mixed,
    a_ssem, a_rsem, c_ssem, c_rsem, h_ssem, h_rsem, e_ssem, e_rsem, m_ssem, m_rsem, d_ssem, d_rsem, l_sem, i_sem,
):
    t = lax.axis_index("tile")
    l = lax.axis_index("lev")
    div, rem = lax.div, lax.rem
    ring = div(t, 8)
    yc = rem(t, 8)
    hi = div(ring, 4)
    x = rem(ring, 4)
    z = hi * 4 + l
    group = rem(l + 2, 4)
    eighth = div(rem(z + 6, 8), 4) * 4 + x

    def at(zz, xx):
        return {"tile": (div(zz, 4) * 4 + xx) * 8 + yc, "lev": rem(zz, 4)}

    low = {"tile": ring * 8 + rem(yc + 7, 8), "lev": l}
    high = {"tile": ring * 8 + rem(yc + 1, 8), "lev": l}

    pending = {}

    def begin(key, start, sent, arrived):
        start()
        pending[key] = [arrived, sent]

    def left(*keys):
        for key in keys:
            pending[key][1]()
            pending[key][1] = lambda: None

    def arrive(*keys):
        for key in keys:
            pending[key][0]()
            pending[key][0] = None

    barrier = pltpu.get_barrier_semaphore()
    greeted = [at(rem(z + dz, 8), rem(x + dx, 4)) for dz in (2, 6) for dx in range(4)]
    greeted += [at(rem(z + 1, 8), x), at(rem(z + 7, 8), x), low, high]
    for device in greeted:
        pl.semaphore_signal(barrier, inc=1, device_id=device, device_id_type=MESH)
    x_load = pltpu.make_async_copy(x_ref.at[0], x_vmem, i_sem.at[0])
    w_load = pltpu.make_async_copy(w_ref.at[0], w_vmem, i_sem.at[1])
    x_load.start()
    w_load.start()

    flip_i = f_ref[0, 0]
    flip_j = f_ref[0, 1]
    c_tmp[...] = jnp.zeros((128, 128), jnp.float32)
    for i in range(8):
        c_tmp[8 * i:8 * i + 8, 0:LEV] = c1_ref[0, i]
        c_tmp[64 + 8 * i:72 + 8 * i, 0:LEV] = c2_ref[0, i]
    turned = c_tmp[...].T
    c_send[...] = turned[0:24]
    c_send[18:19, :] = jnp.full((1, 128), flip_i, jnp.int32).astype(jnp.float32)
    c_send[19:20, :] = jnp.full((1, 128), flip_j, jnp.int32).astype(jnp.float32)

    x_load.wait()
    turn = jnp.full((8, 128), flip_j, jnp.int32) == 1

    def pack(n, carry):
        levels = [2 * n, 2 * n + 1]
        for lev in levels:
            for i in range(8):
                fb[SUBSTEPS - 1, lev, pl.ds(i, 8, stride=8), :] = x_vmem[i + flip_i * (7 - 2 * i), lev]
        for lev in levels:
            rows = [fb[SUBSTEPS - 1, lev, 8 * j:8 * j + 8, :] for j in range(8)]
            rows = [jnp.where(turn, rows[7 - j], rows[j]) for j in range(8)]
            for d, v in enumerate(pick_blocks(turn_blocks(rows))):
                send[d, lev] = v
        return carry

    lax.fori_loop(0, LEV // 2, pack, 0)

    pl.semaphore_wait(barrier, len(greeted))

    def block_of(zz, xx):
        return div(rem(zz + 6, 8), 4) * 4 + xx

    def ring_copy(o, sending):
        dz, dx = (2, 6)[o // 4], o % 4
        if sending:
            return rem(z + dz, 8), rem(x + dx, 4), ring
        zs, xs = rem(z + 8 - dz, 8), rem(x + 4 - dx, 4)
        return zs, xs, div(zs, 4) * 4 + xs

    def c_copy(o, sending=True):
        zz, xx, slot = ring_copy(o, sending)
        return pltpu.make_async_remote_copy(
            src_ref=c_send, dst_ref=c_recv.at[pl.ds(slot * 24, 24)],
            send_sem=c_ssem.at[o], recv_sem=c_rsem.at[o], device_id=at(zz, xx), device_id_type=MESH)

    def a_copy(o, ch, sending=True):
        first, count = CHUNKS[ch]
        zz, xx, slot = ring_copy(o, sending)
        return pltpu.make_async_remote_copy(
            src_ref=send.at[block_of(zz, xx), pl.ds(first, count)], dst_ref=recv.at[slot, pl.ds(first, count)],
            send_sem=a_ssem.at[o, ch], recv_sem=a_rsem.at[o, ch], device_id=at(zz, xx), device_id_type=MESH)

    order = [0, 4, 1, 5, 2, 6, 3, 7]
    for o in order:
        begin(("c", o), c_copy(o).start, c_copy(o).wait_send, c_copy(o, False).wait_recv)
    def exchange(ch):
        for o in order:
            begin(("a", ch, o), a_copy(o, ch).start, a_copy(o, ch).wait_send, a_copy(o, ch, False).wait_recv)

    exchange(0)
    w_load.wait()
    diagonal = jnp.where(
        lax.broadcasted_iota(jnp.int32, (72, 72), 0) == lax.broadcasted_iota(jnp.int32, (72, 72), 1), 0.6, 0.0)

    def prepare(cell, carry):
        s, j = cell // 8, cell % 8
        w = w_vmem[s, j]
        total = jnp.sum(w, axis=-1, keepdims=True)
        matrix[cell] = 0.4 * (w / total) + diagonal
        return carry

    lax.fori_loop(0, 16, prepare, 0)
    left(*(("a", 0, o) for o in range(8)))
    exchange(1)

    arrive(*(("c", o) for o in range(8)))
    spread = (
        lax.broadcasted_iota(jnp.int32, (24, 128), 0) % 8 == lax.broadcasted_iota(jnp.int32, (24, 128), 1) // 16
    ).astype(jnp.float32).astype(jnp.bfloat16)

    def spread_level(lev):
        v = c_recv[pl.ds(lev, 8, stride=24), :]
        p0 = v.astype(jnp.bfloat16).astype(jnp.float32)
        p1 = (v - p0).astype(jnp.bfloat16).astype(jnp.float32)
        p2 = v - p0 - p1
        parts = jnp.concatenate([p0, p1, p2], axis=0).astype(jnp.bfloat16)
        return lax.dot_general(parts, spread, (((0,), (0,)), ((), ())), preferred_element_type=jnp.float32)

    def courant(n, carry):
        levels = [3 * n + u for u in range(3)]
        for u, lev in enumerate(levels):
            wide = spread_level(lev)
            for i in range(8):
                for n, value in enumerate(coefficients(wide[8 * i:8 * i + 8])):
                    k1[n, lev, 8 * i + 8:8 * i + 16, :] = value
                    if i == 7:
                        k1[n, lev, 0:8, :] = pltpu.roll(value, 16, 1)
                raw[u, pl.ds(i, 8, stride=8), :] = wide[64 + 8 * i:72 + 8 * i]
        for u, lev in enumerate(levels):
            for j in range(8):
                for n, value in enumerate(coefficients(raw[u, 8 * j:8 * j + 8, :])):
                    k2[n, lev, 8 * j + 8:8 * j + 16, :] = value
            edge_send[lev] = raw[u, 56:64, :]
        return carry

    lax.fori_loop(0, LEV // 3, courant, 0)
    for n in range(2):
        flags[n] = spread_level(18 + n)[0:8]

    edge = pltpu.make_async_remote_copy(
        src_ref=edge_send, dst_ref=edge_recv, send_sem=e_ssem, recv_sem=e_rsem, device_id=high, device_id_type=MESH)
    left(*(("a", 1, o) for o in range(8)))
    exchange(2)
    begin("edge", edge.start, edge.wait_send, edge.wait_recv)

    roll_low = jnp.where(yc == 0, 16, 0)
    roll_high = jnp.where(yc == 7, 112, 0)
    arrival_turn = [16 * rem(slot + 8 - eighth, 8) for slot in range(8)]
    column_turn = [16 * rem(slot + 8 - ring, 8) for slot in range(8)]

    def unpack(ch):
        first, count = CHUNKS[ch]
        arrive(*(("a", ch, o) for o in range(8)))

        def some(n, carry):
            levels = [first + 2 * n, first + 2 * n + 1]
            for lev in levels:
                rows = pick_blocks([pltpu.roll(recv[slot, lev], arrival_turn[slot], 1) for slot in range(8)])
                for j, v in enumerate(turn_back(rows)):
                    fa[lev, pl.ds(j, 8, stride=8), :] = v
            return carry

        lax.fori_loop(0, count // 2, some, 0)

    def advance(q, low_cells, high_cells, k, lev):
        e = low_cells + q + high_cells
        a = [face_value(*e[n:n + 4]) for n in range(11)]
        flux = [
            face_flux(a[f + 1], a[f], a[f + 2], e[f + 2], e[f + 3], *(k[n, lev, 8 * f:8 * f + 8, :] for n in range(3)))
            for f in range(9)]
        return [q[n] - (flux[n + 1] - flux[n]) for n in range(8)]

    def sweep_first(step, ch):
        first, count = CHUNKS[ch]

        def level(lev):
            q = [fa[lev, 8 * i:8 * i + 8, :] for i in range(8)]
            return advance(q, [pltpu.roll(v, 16, 1) for v in q[5:]], [pltpu.roll(v, 112, 1) for v in q[:3]], k1, lev)

        def some(n, carry):
            levels = [first + n * UNROLL + k for k in range(UNROLL)]
            new = [level(lev) for lev in levels]
            for lev, rows in zip(levels, new):
                for i in range(8):
                    fb[step, lev, pl.ds(i, 8, stride=8), :] = rows[i]
            return carry

        lax.fori_loop(0, count // UNROLL, some, 0)

    def halo_copies(step, ch):
        first, count = CHUNKS[ch]
        return (
            pltpu.make_async_remote_copy(
                src_ref=fb.at[step, pl.ds(first, count), pl.ds(40, 24)], dst_ref=halo_low.at[step, pl.ds(first, count)],
                send_sem=h_ssem.at[0, step, ch], recv_sem=h_rsem.at[0, step, ch], device_id=high, device_id_type=MESH),
            pltpu.make_async_remote_copy(
                src_ref=fb.at[step, pl.ds(first, count), pl.ds(0, 24)], dst_ref=halo_high.at[step, pl.ds(first, count)],
                send_sem=h_ssem.at[1, step, ch], recv_sem=h_rsem.at[1, step, ch], device_id=low, device_id_type=MESH),
        )

    def sweep_second(step, ch):
        first, count = CHUNKS[ch]
        last = step == SUBSTEPS - 1

        def level(lev):
            q = [fb[step, lev, 8 * j:8 * j + 8, :] for j in range(8)]
            new = advance(
                q, [pltpu.roll(halo_low[step, lev, 8 * j:8 * j + 8, :], roll_low, 1) for j in range(3)],
                [pltpu.roll(halo_high[step, lev, 8 * j:8 * j + 8, :], roll_high, 1) for j in range(3)], k2, lev)
            if last:
                back = flags[1] > 0.5
                new = [jnp.where(back, new[7 - j], new[j]) for j in range(8)]
            return new

        def some(n, carry):
            levels = [first + n * UNROLL + k for k in range(UNROLL)]
            new = [level(lev) for lev in levels]
            for lev, rows in zip(levels, new):
                for j in range(8):
                    fa[lev, pl.ds(j, 8, stride=8), :] = rows[j]
            return carry

        lax.fori_loop(0, count // UNROLL, some, 0)

    def edge_levels(n, carry):
        for lev in [6 * n + u for u in range(6)]:
            for n, value in enumerate(coefficients(pltpu.roll(edge_recv[lev], roll_low, 1))):
                k2[n, lev, 0:8, :] = value
        return carry

    def mix_pack(ch):
        groups = GROUPS[ch]

        def one(r, carry):
            back = flags[0] > 0.5
            for m in groups:
                rows = []
                for k in range(8):
                    lev, i = 4 * m + k // 2, 2 * r + k % 2
                    if lev < LEV:
                        here = fa[lev, pl.ds(pl.multiple_of(8 * i, 8), 8), :]
                        there = fa[lev, pl.ds(pl.multiple_of(56 - 8 * i, 8), 8), :]
                        rows.append(jnp.where(back, there, here))
                    else:
                        rows.append(jnp.zeros((8, 128), jnp.float32))
                for k, v in enumerate(pick_blocks(turn_blocks(rows))):
                    mix_send[k * 4 + r, m] = v
            return carry

        lax.fori_loop(0, 4, one, 0)

    def m_copy(o, ch):
        zd, xd = rem(z + div(o, 4), 8), rem(x + rem(o, 4), 4)
        part = pl.ds(GROUPS[ch][0], len(GROUPS[ch]))
        return pltpu.make_async_remote_copy(
            src_ref=mix_send.at[(div(zd, 4) * 4 + xd) * 4 + rem(zd, 4), part], dst_ref=mix_recv.at[group * 8 + eighth, part],
            send_sem=m_ssem.at[ch, o], recv_sem=m_rsem.at[ch, o], device_id=at(zd, xd), device_id_type=MESH)

    def m_arrival(o, ch):
        zs, xs = rem(z + 8 - div(o, 4), 8), rem(x + 4 - rem(o, 4), 4)
        slot = rem(zs + 2, 4) * 8 + block_of(zs, xs)
        part = pl.ds(GROUPS[ch][0], len(GROUPS[ch]))
        return pltpu.make_async_remote_copy(
            src_ref=mix_send.at[0, part], dst_ref=mix_recv.at[slot, part],
            send_sem=m_ssem.at[ch, o], recv_sem=m_rsem.at[ch, o], device_id=at(zs, xs), device_id_type=MESH)

    own = [
        pltpu.make_async_copy(
            mix_send.at[ring * 4 + l, pl.ds(groups[0], len(groups))],
            mix_recv.at[group * 8 + eighth, pl.ds(groups[0], len(groups))], l_sem.at[2 + ch])
        for ch, groups in enumerate(GROUPS)
    ]

    def segment(step, ch):
        if step == 0:
            unpack(ch)
        else:
            arrive(("h", step - 1, ch, 0), ("h", step - 1, ch, 1))
            sweep_second(step - 1, ch)
        if step < SUBSTEPS:
            sweep_first(step, ch)
            for side, copy in enumerate(halo_copies(step, ch)):
                begin(("h", step, ch, side), copy.start, copy.wait_send, copy.wait_recv)
            return
        mix_pack(ch)

        def others(action):
            def run():
                def one(o, carry):
                    action(o)
                    return carry

                lax.fori_loop(1, 32, one, 0)

            return run

        begin(
            ("m", ch), others(lambda o: m_copy(o, ch).start()),
            others(lambda o: m_copy(o, ch).wait_send()), others(lambda o: m_arrival(o, ch).wait_recv()))
        begin(("own", ch), own[ch].start, lambda: None, own[ch].wait)

    for wave in range(SUBSTEPS + NCH):
        if wave == 1:
            arrive("edge")
            lax.fori_loop(0, LEV // 6, edge_levels, 0)
        for ch in range(NCH):
            if 0 <= wave - ch <= SUBSTEPS:
                segment(wave - ch, ch)

    for ch in range(NCH):
        arrive(("m", ch), ("own", ch))

    def mix_unpack(g, carry):
        for m in range(5):
            rows = pick_blocks([pltpu.roll(mix_recv[g * 8 + k, m], column_turn[k], 1) for k in range(8)])
            rows = turn_back(rows)
            for k in range(8):
                lev, s = 4 * m + k // 2, k % 2
                if lev < LEV:
                    columns[s, pl.ds(pl.multiple_of((g * LEV + lev) * 8, 8), 8), :] = rows[k]
        return carry

    lax.fori_loop(0, 4, mix_unpack, 0)

    def d_copy(s, o):
        to = rem(l + o, 4)
        return pltpu.make_async_remote_copy(
            src_ref=mixed.at[s, pl.ds(to * 144, 144)], dst_ref=o_ref.at[0, 2 * l + s],
            send_sem=d_ssem.at[s, o], recv_sem=d_rsem.at[s, o], device_id={"tile": t, "lev": to}, device_id_type=MESH)

    def d_arrival(s, o):
        source = rem(l + 4 - o, 4)
        return pltpu.make_async_remote_copy(
            src_ref=mixed.at[s, pl.ds(0, 144)], dst_ref=o_ref.at[0, 2 * source + s],
            send_sem=d_ssem.at[s, o], recv_sem=d_rsem.at[s, o], device_id={"tile": t, "lev": source}, device_id_type=MESH)

    def mix_row(s):
        def one(j, carry):
            v = columns[s, pl.ds(j, 72, stride=8), :]
            v_hi = v.astype(jnp.bfloat16)
            v_lo = (v - v_hi.astype(jnp.float32)).astype(jnp.bfloat16)
            m = matrix[s * 8 + j]
            m_hi = m.astype(jnp.bfloat16)
            m_lo = (m - m_hi.astype(jnp.float32)).astype(jnp.bfloat16)
            dot = lambda a, b: jnp.dot(a, b, preferred_element_type=jnp.float32)
            out = dot(m_hi, v_hi) + (dot(m_hi, v_lo) + dot(m_lo, v_hi))
            mixed[s, pl.ds(j, 72, stride=8), :] = out
            return carry

        lax.fori_loop(0, 8, one, 0)

    for s in range(2):
        mix_row(s)
        for o in range(1, 4):
            begin(("d", s, o), d_copy(s, o).start, d_copy(s, o).wait_send, d_arrival(s, o).wait_recv)
        local = pltpu.make_async_copy(mixed.at[s, pl.ds(l * 144, 144)], o_ref.at[0, 2 * l + s], l_sem.at[s])
        begin(("local", s), local.start, lambda: None, local.wait)

    for arrived, sent in pending.values():
        if arrived is not None:
            arrived()
        sent()


def solution(mesh):
    f32 = jnp.float32

    def on_device(tracers, courant_first, courant_second, weights, frame_flip):
        vmem = pl.BlockSpec(memory_space=pltpu.VMEM)
        hbm = pl.BlockSpec(memory_space=pl.ANY)
        dma = pltpu.SemaphoreType.DMA
        rows = jnp.transpose(tracers, (0, 1, 3, 2, 4)).reshape(1, 8, LEV, 8, 128)
        out = pl.pallas_call(
            kernel,
            out_shape=jax.ShapeDtypeStruct((1, 8, LEV * 8, 128), f32),
            in_specs=[hbm, vmem, vmem, hbm, pl.BlockSpec(memory_space=pltpu.SMEM)],
            out_specs=vmem,
            scratch_shapes=[
                pltpu.VMEM((8, LEV, 8, 128), f32),
                pltpu.VMEM((2, 8, 72, 72), f32),
                pltpu.VMEM((8, LEV, 8, 128), f32),
                pltpu.VMEM((8, LEV, 8, 128), f32),
                pltpu.VMEM((128, 128), f32),
                pltpu.VMEM((24, 128), f32),
                pltpu.VMEM((192, 128), f32),
                pltpu.VMEM((3, 64, 128), f32),
                pltpu.VMEM((2, 8, 128), f32),
                pltpu.VMEM((LEV, 64, 128), f32),
                pltpu.VMEM((SUBSTEPS, LEV, 64, 128), f32),
                pltpu.VMEM((SUBSTEPS, LEV, 24, 128), f32),
                pltpu.VMEM((SUBSTEPS, LEV, 24, 128), f32),
                pltpu.VMEM((LEV, 8, 128), f32),
                pltpu.VMEM((LEV, 8, 128), f32),
                pltpu.VMEM((3, LEV, 72, 128), f32),
                pltpu.VMEM((3, LEV, 72, 128), f32),
                pltpu.VMEM((32, 5, 8, 128), f32),
                pltpu.VMEM((32, 5, 8, 128), f32),
                pltpu.VMEM((2, 72 * 8, 128), f32),
                pltpu.VMEM((16, 72, 72), f32),
                pltpu.VMEM((2, 72 * 8, 128), f32),
                dma((8, NCH)), dma((8, NCH)),
                dma((8,)), dma((8,)),
                dma((2, SUBSTEPS, NCH)), dma((2, SUBSTEPS, NCH)),
                dma, dma,
                dma((NCH, 32)), dma((NCH, 32)),
                dma((2, 4)), dma((2, 4)),
                dma((2 + NCH,)),
                dma((2,)),
            ],
            compiler_params=pltpu.CompilerParams(collective_id=0, has_side_effects=True),
        )(rows, courant_first, courant_second, weights, frame_flip)
        return jnp.transpose(out.reshape(1, 8, LEV, 8, 128), (0, 1, 3, 2, 4))

    return jax.shard_map(
        on_device,
        mesh=mesh,
        in_specs=(
            P("tile", None, None, "lev", None),
            P("tile", None, None, "lev"),
            P("tile", None, None, "lev"),
            P("tile", "lev", None, None, None),
            P("tile", None),
        ),
        out_specs=P("tile", None, None, "lev", None),
        check_vma=False,
    )
```

time: 83.5 us -> 74.9 us (0.90)
  Pallas kernels: 81.4 us -> 72.7 us
    pallas_call x1, Pallas kernels: 81.4 us -> 72.7 us  [on_device(): pl.pallas_call(kernel, out_shape=jax.ShapeDtypeStruct((1, 8, LEV * 8, 128...]
where the time goes in v3:
time: 74.9 us; the launch traced here: 74.7 us
  Pallas kernels  72.7 us (97%)
  local copies, waits for them, and re-layouts  1.92 us (3%)
    pallas_call x1, Pallas kernels, on_device(): pl.pallas_call(kernel, out_shape=jax.ShapeDtypeStruct((1, 8, LEV * 8, 128...  72.7 us
    unnamed x1, local copies, waits for them, and re-layouts  1.92 us

profile of v3, /device:TPU:41, one launch (start us, length us, event | category | flops | bytes accessed | tf_op | source)
XLA Modules:
  0.0 74.7 jit_solution(3064867973234739524)
XLA Ops:
  0.0 72.7 %shard_map.55 = f32[1,8,144,128]{3,2,1,0:T(8,128)} custom-call(f32[1,8,18,8,128]{4,3,2,1,0:T(8,128)} %bitcast.5, f32[1,8,8,18]{3,2,1,0:T(8,128)} %c1_ref.1, f32[1,8,8,18]{3,2,1,0:T(8,128)} %c2_ref.1, f32[1,2,8,72,72]{4,3,2,1,0:T(8,128)} %w_ref.1, s32[1,2]{1,0:T(1,128)} %f_ref.1), custom_call_target="tpu_custom_call" | custom-call | tf_op jit(solution)/shard_map/pallas_call | solution.py:445
  72.7 1.9 %copy.7 = f32[1,8,8,18,128]{4,2,3,1,0:T(8,128)} copy(f32[1,8,8,18,128]{4,2,3,1,0:T(8,128)} %bitcast.4) | data formatting | bytes 1179648

commit v4 on v3

--- a/solution.py
+++ b/solution.py
@@ -1,3 +1,5 @@
+import functools
+
 import jax
 import jax.numpy as jnp
 from jax import lax
@@ -10,6 +12,11 @@
 LEV = 18
 CHUNKS = ((0, 8), (8, 4), (12, 6))
 NCH = len(CHUNKS)
+SCHEDULE = (
+    ("courant", 0), ("send", 1), ("step", 0, 0), ("courant", 1), ("send", 2), ("step", 1, 0), ("step", 0, 1),
+    ("courant", 2), ("flags", 0), ("step", 1, 1), ("step", 0, 2), ("step", 2, 0), ("step", 1, 2), ("step", 0, 3),
+    ("scatter", 0), ("step", 2, 1), ("step", 1, 3), ("scatter", 1), ("step", 2, 2), ("step", 2, 3), ("scatter", 2),
+)
 GROUPS = tuple(tuple(range(first // 4, (first + count + 3) // 4)) for first, count in CHUNKS)
 UNROLL = 2
 
@@ -172,8 +179,6 @@
         return carry
 
     lax.fori_loop(0, 16, prepare, 0)
-    left(*(("a", 0, o) for o in range(8)))
-    exchange(1)
 
     arrive(*(("c", o) for o in range(8)))
     spread = (
@@ -188,8 +193,8 @@
         parts = jnp.concatenate([p0, p1, p2], axis=0).astype(jnp.bfloat16)
         return lax.dot_general(parts, spread, (((0,), (0,)), ((), ())), preferred_element_type=jnp.float32)
 
-    def courant(n, carry):
-        levels = [3 * n + u for u in range(3)]
+    def courant(first, width, n, carry):
+        levels = [first + width * n + u for u in range(width)]
         for u, lev in enumerate(levels):
             wide = spread_level(lev)
             for i in range(8):
@@ -205,15 +210,18 @@
             edge_send[lev] = raw[u, 56:64, :]
         return carry
 
-    lax.fori_loop(0, LEV // 3, courant, 0)
-    for n in range(2):
-        flags[n] = spread_level(18 + n)[0:8]
-
-    edge = pltpu.make_async_remote_copy(
-        src_ref=edge_send, dst_ref=edge_recv, send_sem=e_ssem, recv_sem=e_rsem, device_id=high, device_id_type=MESH)
-    left(*(("a", 1, o) for o in range(8)))
-    exchange(2)
-    begin("edge", edge.start, edge.wait_send, edge.wait_recv)
+    def edge_copy(ch):
+        part = pl.ds(*CHUNKS[ch])
+        return pltpu.make_async_remote_copy(
+            src_ref=edge_send.at[part], dst_ref=edge_recv.at[part],
+            send_sem=e_ssem.at[ch], recv_sem=e_rsem.at[ch], device_id=high, device_id_type=MESH)
+
+    def courant_chunk(ch):
+        first, count = CHUNKS[ch]
+        width = 3 if count % 3 == 0 else 2
+        lax.fori_loop(0, count // width, functools.partial(courant, first, width), 0)
+        edge = edge_copy(ch)
+        begin(("e", ch), edge.start, edge.wait_send, edge.wait_recv)
 
     roll_low = jnp.where(yc == 0, 16, 0)
     roll_high = jnp.where(yc == 7, 112, 0)
@@ -294,11 +302,17 @@
 
         lax.fori_loop(0, count // UNROLL, some, 0)
 
-    def edge_levels(n, carry):
-        for lev in [6 * n + u for u in range(6)]:
-            for n, value in enumerate(coefficients(pltpu.roll(edge_recv[lev], roll_low, 1))):
-                k2[n, lev, 0:8, :] = value
-        return carry
+    def edge_chunk(ch):
+        first, count = CHUNKS[ch]
+        arrive(("e", ch))
+
+        def some(n, carry):
+            for lev in [first + 2 * n, first + 2 * n + 1]:
+                for n, value in enumerate(coefficients(pltpu.roll(edge_recv[lev], roll_low, 1))):
+                    k2[n, lev, 0:8, :] = value
+            return carry
+
+        lax.fori_loop(0, count // 2, some, 0)
 
     def mix_pack(ch):
         groups = GROUPS[ch]
@@ -322,7 +336,8 @@
         lax.fori_loop(0, 4, one, 0)
 
     def m_copy(o, ch):
-        zd, xd = rem(z + div(o, 4), 8), rem(x + rem(o, 4), 4)
+        dz, dx = (o // 4, o % 4) if isinstance(o, int) else (div(o, 4), rem(o, 4))
+        zd, xd = rem(z + dz, 8), rem(x + dx, 4)
         part = pl.ds(GROUPS[ch][0], len(GROUPS[ch]))
         return pltpu.make_async_remote_copy(
             src_ref=mix_send.at[(div(zd, 4) * 4 + xd) * 4 + rem(zd, 4), part], dst_ref=mix_recv.at[group * 8 + eighth, part],
@@ -347,37 +362,52 @@
         if step == 0:
             unpack(ch)
         else:
+            if step == 1:
+                edge_chunk(ch)
             arrive(("h", step - 1, ch, 0), ("h", step - 1, ch, 1))
             sweep_second(step - 1, ch)
         if step < SUBSTEPS:
             sweep_first(step, ch)
             for side, copy in enumerate(halo_copies(step, ch)):
                 begin(("h", step, ch, side), copy.start, copy.wait_send, copy.wait_recv)
-            return
+
+    def others(action):
+        def run():
+            def one(o, carry):
+                action(o)
+                return carry
+
+            lax.fori_loop(1, 32, one, 0)
+
+        return run
+
+    def scatter(ch):
         mix_pack(ch)
 
-        def others(action):
-            def run():
-                def one(o, carry):
-                    action(o)
-                    return carry
-
-                lax.fori_loop(1, 32, one, 0)
-
-            return run
+        def far_first():
+            for dz in (4, 3, 5, 2, 6, 1, 7, 0):
+                for dx in (2, 1, 3, 0):
+                    if dz or dx:
+                        m_copy(4 * dz + dx, ch).start()
 
         begin(
-            ("m", ch), others(lambda o: m_copy(o, ch).start()),
+            ("m", ch), far_first,
             others(lambda o: m_copy(o, ch).wait_send()), others(lambda o: m_arrival(o, ch).wait_recv()))
         begin(("own", ch), own[ch].start, lambda: None, own[ch].wait)
 
-    for wave in range(SUBSTEPS + NCH):
-        if wave == 1:
-            arrive("edge")
-            lax.fori_loop(0, LEV // 6, edge_levels, 0)
-        for ch in range(NCH):
-            if 0 <= wave - ch <= SUBSTEPS:
-                segment(wave - ch, ch)
+    for what, ch, *step in SCHEDULE:
+        if what == "send":
+            left(*(("a", ch - 1, o) for o in range(8)))
+            exchange(ch)
+        elif what == "flags":
+            for n in range(2):
+                flags[n] = spread_level(LEV + n)[0:8]
+        elif what == "courant":
+            courant_chunk(ch)
+        elif what == "scatter":
+            scatter(ch)
+        else:
+            segment(step[0], ch)
 
     for ch in range(NCH):
         arrive(("m", ch), ("own", ch))
@@ -473,7 +503,7 @@
                 dma((8, NCH)), dma((8, NCH)),
                 dma((8,)), dma((8,)),
                 dma((2, SUBSTEPS, NCH)), dma((2, SUBSTEPS, NCH)),
-                dma, dma,
+                dma((NCH,)), dma((NCH,)),
                 dma((NCH, 32)), dma((NCH, 32)),
                 dma((2, 4)), dma((2, 4)),
                 dma((2 + NCH,)),

time: 74.9 us -> 72.9 us (0.973)
  Pallas kernels: 72.7 us -> 70.3 us
    pallas_call x1, Pallas kernels: 72.7 us -> 70.3 us  [on_device(): pl.pallas_call(kernel, out_shape=jax.ShapeDtypeStruct((1, 8, LEV * 8, 128...]
where the time goes in v4:
time: 72.9 us; the launch traced here: 72.3 us
  Pallas kernels  70.3 us (96%)
  local copies, waits for them, and re-layouts  1.92 us (3%)
    pallas_call x1, Pallas kernels, on_device(): pl.pallas_call(kernel, out_shape=jax.ShapeDtypeStruct((1, 8, LEV * 8, 128...  70.3 us
    unnamed x1, local copies, waits for them, and re-layouts  1.92 us

profile of v4, /device:TPU:41, one launch (start us, length us, event | category | flops | bytes accessed | tf_op | source)
XLA Modules:
  0.0 72.3 jit_solution(12856956806045657093)
XLA Ops:
  0.0 70.3 %shard_map.55 = f32[1,8,144,128]{3,2,1,0:T(8,128)} custom-call(f32[1,8,18,8,128]{4,3,2,1,0:T(8,128)} %bitcast.5, f32[1,8,8,18]{3,2,1,0:T(8,128)} %c1_ref.1, f32[1,8,8,18]{3,2,1,0:T(8,128)} %c2_ref.1, f32[1,2,8,72,72]{4,3,2,1,0:T(8,128)} %w_ref.1, s32[1,2]{1,0:T(1,128)} %f_ref.1), custom_call_target="tpu_custom_call" | custom-call | tf_op jit(solution)/shard_map/pallas_call | solution.py:475
  70.3 1.9 %copy.7 = f32[1,8,8,18,128]{4,2,3,1,0:T(8,128)} copy(f32[1,8,8,18,128]{4,2,3,1,0:T(8,128)} %bitcast.4) | data formatting | bytes 1179648

commit v5 on v4

--- a/solution.py
+++ b/solution.py
@@ -13,12 +13,13 @@
 CHUNKS = ((0, 8), (8, 4), (12, 6))
 NCH = len(CHUNKS)
 SCHEDULE = (
-    ("courant", 0), ("send", 1), ("step", 0, 0), ("courant", 1), ("send", 2), ("step", 1, 0), ("step", 0, 1),
-    ("courant", 2), ("flags", 0), ("step", 1, 1), ("step", 0, 2), ("step", 2, 0), ("step", 1, 2), ("step", 0, 3),
-    ("scatter", 0), ("step", 2, 1), ("step", 1, 3), ("scatter", 1), ("step", 2, 2), ("step", 2, 3), ("scatter", 2),
+    ("courant", 0), ("send", 1), ("step", 0, 0), ("courant", 1), ("send", 2), ("courant", 2), ("flags", 0),
+    ("step", 0, 1), ("step", 1, 0), ("step", 0, 2), ("step", 1, 1), ("step", 2, 0), ("step", 0, 3), ("scatter", 0),
+    ("step", 1, 2), ("step", 2, 1), ("step", 1, 3), ("scatter", 1), ("step", 2, 2), ("step", 2, 3), ("scatter", 2),
 )
 GROUPS = tuple(tuple(range(first // 4, (first + count + 3) // 4)) for first, count in CHUNKS)
 UNROLL = 2
+CELLS = 4
 
 
 def turn_blocks(rows):
@@ -409,20 +410,22 @@
         else:
             segment(step[0], ch)
 
+    def mix_unpack(ch):
+        def one(g, carry):
+            for m in GROUPS[ch]:
+                rows = pick_blocks([pltpu.roll(mix_recv[g * 8 + k, m], column_turn[k], 1) for k in range(8)])
+                rows = turn_back(rows)
+                for k in range(8):
+                    lev, s = 4 * m + k // 2, k % 2
+                    if lev < LEV:
+                        columns[s, pl.ds(pl.multiple_of((g * LEV + lev) * 8, 8), 8), :] = rows[k]
+            return carry
+
+        lax.fori_loop(0, 4, one, 0)
+
     for ch in range(NCH):
         arrive(("m", ch), ("own", ch))
-
-    def mix_unpack(g, carry):
-        for m in range(5):
-            rows = pick_blocks([pltpu.roll(mix_recv[g * 8 + k, m], column_turn[k], 1) for k in range(8)])
-            rows = turn_back(rows)
-            for k in range(8):
-                lev, s = 4 * m + k // 2, k % 2
-                if lev < LEV:
-                    columns[s, pl.ds(pl.multiple_of((g * LEV + lev) * 8, 8), 8), :] = rows[k]
-        return carry
-
-    lax.fori_loop(0, 4, mix_unpack, 0)
+        mix_unpack(ch)
 
     def d_copy(s, o):
         to = rem(l + o, 4)
@@ -437,7 +440,7 @@
             send_sem=d_ssem.at[s, o], recv_sem=d_rsem.at[s, o], device_id={"tile": t, "lev": source}, device_id_type=MESH)
 
     def mix_row(s):
-        def one(j, carry):
+        def cell(j):
             v = columns[s, pl.ds(j, 72, stride=8), :]
             v_hi = v.astype(jnp.bfloat16)
             v_lo = (v - v_hi.astype(jnp.float32)).astype(jnp.bfloat16)
@@ -447,13 +450,17 @@
             dot = lambda a, b: jnp.dot(a, b, preferred_element_type=jnp.float32)
             out = dot(m_hi, v_hi) + (dot(m_hi, v_lo) + dot(m_lo, v_hi))
             mixed[s, pl.ds(j, 72, stride=8), :] = out
-            return carry
-
-        lax.fori_loop(0, 8, one, 0)
+
+        def some(n, carry):
+            for j in range(CELLS):
+                cell(CELLS * n + j)
+            return carry
+
+        lax.fori_loop(0, 8 // CELLS, some, 0)
 
     for s in range(2):
         mix_row(s)
-        for o in range(1, 4):
+        for o in (2, 3, 1):
             begin(("d", s, o), d_copy(s, o).start, d_copy(s, o).wait_send, d_arrival(s, o).wait_recv)
         local = pltpu.make_async_copy(mixed.at[s, pl.ds(l * 144, 144)], o_ref.at[0, 2 * l + s], l_sem.at[s])
         begin(("local", s), local.start, lambda: None, local.wait)
@@ -476,7 +483,7 @@
             kernel,
             out_shape=jax.ShapeDtypeStruct((1, 8, LEV * 8, 128), f32),
             in_specs=[hbm, vmem, vmem, hbm, pl.BlockSpec(memory_space=pltpu.SMEM)],
-            out_specs=vmem,
+            out_specs=hbm,
             scratch_shapes=[
                 pltpu.VMEM((8, LEV, 8, 128), f32),
                 pltpu.VMEM((2, 8, 72, 72), f32),

time: 72.9 us -> 70.9 us (0.973)
  Pallas kernels: 70.3 us -> 68.7 us
    pallas_call x1, Pallas kernels: 70.3 us -> 68.7 us  [on_device(): pl.pallas_call(kernel, out_shape=jax.ShapeDtypeStruct((1, 8, LEV * 8, 128...]
where the time goes in v5:
time: 70.9 us; the launch traced here: 70.7 us
  Pallas kernels  68.7 us (97%)
  local copies, waits for them, and re-layouts  1.92 us (3%)
    pallas_call x1, Pallas kernels, on_device(): pl.pallas_call(kernel, out_shape=jax.ShapeDtypeStruct((1, 8, LEV * 8, 128...  68.7 us
    unnamed x1, local copies, waits for them, and re-layouts  1.92 us

profile of v5, /device:TPU:41, one launch (start us, length us, event | category | flops | bytes accessed | tf_op | source)
XLA Modules:
  0.0 70.7 jit_solution(18121222492021761069)
XLA Ops:
  0.0 68.7 %shard_map.55 = f32[1,8,144,128]{3,2,1,0:T(8,128)} custom-call(f32[1,8,18,8,128]{4,3,2,1,0:T(8,128)} %bitcast.5, f32[1,8,8,18]{3,2,1,0:T(8,128)} %c1_ref.1, f32[1,8,8,18]{3,2,1,0:T(8,128)} %c2_ref.1, f32[1,2,8,72,72]{4,3,2,1,0:T(8,128)} %w_ref.1, s32[1,2]{1,0:T(1,128)} %f_ref.1), custom_call_target="tpu_custom_call" | custom-call | tf_op jit(solution)/shard_map/pallas_call | solution.py:482
  68.8 1.9 %copy.7 = f32[1,8,8,18,128]{4,2,3,1,0:T(8,128)} copy(f32[1,8,8,18,128]{4,2,3,1,0:T(8,128)} %bitcast.4) | data formatting | bytes 1179648

commit v6 on v5

--- a/solution.py
+++ b/solution.py
@@ -59,7 +59,7 @@
 
 def kernel(
     x_ref, c1_ref, c2_ref, w_ref, f_ref, o_ref,
-    x_vmem, w_vmem, send, recv, c_tmp, c_send, c_recv, raw, flags,
+    x_vmem, c_vmem, w_vmem, send, recv, c_tmp, c_send, c_recv, raw, flags,
     fa, fb, halo_low, halo_high, edge_send, edge_recv,
     k1, k2, mix_send, mix_recv, columns, matrix, mixed,
     a_ssem, a_rsem, c_ssem, c_rsem, h_ssem, h_rsem, e_ssem, e_rsem, m_ssem, m_rsem, d_ssem, d_rsem, l_sem, i_sem,
@@ -104,15 +104,19 @@
         pl.semaphore_signal(barrier, inc=1, device_id=device, device_id_type=MESH)
     x_load = pltpu.make_async_copy(x_ref.at[0], x_vmem, i_sem.at[0])
     w_load = pltpu.make_async_copy(w_ref.at[0], w_vmem, i_sem.at[1])
+    c_load = [pltpu.make_async_copy(ref.at[0], c_vmem.at[n], i_sem.at[2 + n]) for n, ref in enumerate((c1_ref, c2_ref))]
+    c_load[0].start()
+    c_load[1].start()
     x_load.start()
     w_load.start()
 
     flip_i = f_ref[0, 0]
     flip_j = f_ref[0, 1]
     c_tmp[...] = jnp.zeros((128, 128), jnp.float32)
-    for i in range(8):
-        c_tmp[8 * i:8 * i + 8, 0:LEV] = c1_ref[0, i]
-        c_tmp[64 + 8 * i:72 + 8 * i, 0:LEV] = c2_ref[0, i]
+    for n in range(2):
+        c_load[n].wait()
+        for i in range(8):
+            c_tmp[64 * n + 8 * i:64 * n + 8 * i + 8, 0:LEV] = c_vmem[n, i]
     turned = c_tmp[...].T
     c_send[...] = turned[0:24]
     c_send[18:19, :] = jnp.full((1, 128), flip_i, jnp.int32).astype(jnp.float32)
@@ -160,7 +164,7 @@
             src_ref=send.at[block_of(zz, xx), pl.ds(first, count)], dst_ref=recv.at[slot, pl.ds(first, count)],
             send_sem=a_ssem.at[o, ch], recv_sem=a_rsem.at[o, ch], device_id=at(zz, xx), device_id_type=MESH)
 
-    order = [0, 4, 1, 5, 2, 6, 3, 7]
+    order = [2, 6, 1, 5, 3, 7, 0, 4]
     for o in order:
         begin(("c", o), c_copy(o).start, c_copy(o).wait_send, c_copy(o, False).wait_recv)
     def exchange(ch):
@@ -475,17 +479,17 @@
     f32 = jnp.float32
 
     def on_device(tracers, courant_first, courant_second, weights, frame_flip):
-        vmem = pl.BlockSpec(memory_space=pltpu.VMEM)
         hbm = pl.BlockSpec(memory_space=pl.ANY)
         dma = pltpu.SemaphoreType.DMA
         rows = jnp.transpose(tracers, (0, 1, 3, 2, 4)).reshape(1, 8, LEV, 8, 128)
         out = pl.pallas_call(
             kernel,
             out_shape=jax.ShapeDtypeStruct((1, 8, LEV * 8, 128), f32),
-            in_specs=[hbm, vmem, vmem, hbm, pl.BlockSpec(memory_space=pltpu.SMEM)],
+            in_specs=[hbm, hbm, hbm, hbm, pl.BlockSpec(memory_space=pltpu.SMEM)],
             out_specs=hbm,
             scratch_shapes=[
                 pltpu.VMEM((8, LEV, 8, 128), f32),
+                pltpu.VMEM((2, 8, 8, LEV), f32),
                 pltpu.VMEM((2, 8, 72, 72), f32),
                 pltpu.VMEM((8, LEV, 8, 128), f32),
                 pltpu.VMEM((8, LEV, 8, 128), f32),
@@ -514,7 +518,7 @@
                 dma((NCH, 32)), dma((NCH, 32)),
                 dma((2, 4)), dma((2, 4)),
                 dma((2 + NCH,)),
-                dma((2,)),
+                dma((4,)),
             ],
             compiler_params=pltpu.CompilerParams(collective_id=0, has_side_effects=True),
         )(rows, courant_first, courant_second, weights, frame_flip)

time: 70.9 us -> 69.2 us (0.976)
  Pallas kernels: 68.7 us -> 67.1 us
    pallas_call x1, Pallas kernels: 68.7 us -> 67.1 us  [on_device(): pl.pallas_call(kernel, out_shape=jax.ShapeDtypeStruct((1, 8, LEV * 8, 128...]
where the time goes in v6:
time: 69.2 us; the launch traced here: 69 us
  Pallas kernels  67.1 us (97%)
  local copies, waits for them, and re-layouts  1.92 us (3%)
    pallas_call x1, Pallas kernels, on_device(): pl.pallas_call(kernel, out_shape=jax.ShapeDtypeStruct((1, 8, LEV * 8, 128...  67.1 us
    unnamed x1, local copies, waits for them, and re-layouts  1.92 us

profile of v6, /device:TPU:41, one launch (start us, length us, event | category | flops | bytes accessed | tf_op | source)
XLA Modules:
  0.0 69.0 jit_solution(10565159960331242175)
XLA Ops:
  0.0 67.1 %shard_map.55 = f32[1,8,144,128]{3,2,1,0:T(8,128)} custom-call(f32[1,8,18,8,128]{4,3,2,1,0:T(8,128)} %bitcast.5, f32[1,8,8,18]{3,2,1,0:T(8,128)} %c1_ref.1, f32[1,8,8,18]{3,2,1,0:T(8,128)} %c2_ref.1, f32[1,2,8,72,72]{4,3,2,1,0:T(8,128)} %w_ref.1, s32[1,2]{1,0:T(1,128)} %f_ref.1), custom_call_target="tpu_custom_call" | custom-call | tf_op jit(solution)/shard_map/pallas_call | solution.py:485
  67.1 1.9 %copy.7 = f32[1,8,8,18,128]{4,2,3,1,0:T(8,128)} copy(f32[1,8,8,18,128]{4,2,3,1,0:T(8,128)} %bitcast.4) | data formatting | bytes 1179648

commit v7 on v6

--- a/solution.py
+++ b/solution.py
@@ -98,7 +98,7 @@
             pending[key][0] = None
 
     barrier = pltpu.get_barrier_semaphore()
-    greeted = [at(rem(z + dz, 8), rem(x + dx, 4)) for dz in (2, 6) for dx in range(4)]
+    greeted = [at(rem(z + dz, 8), rem(x + dx, 4)) for dx in (2, 1, 3, 0) for dz in (2, 6)]
     greeted += [at(rem(z + 1, 8), x), at(rem(z + 7, 8), x), low, high]
     for device in greeted:
         pl.semaphore_signal(barrier, inc=1, device_id=device, device_id_type=MESH)
@@ -390,10 +390,9 @@
         mix_pack(ch)
 
         def far_first():
-            for dz in (4, 3, 5, 2, 6, 1, 7, 0):
-                for dx in (2, 1, 3, 0):
-                    if dz or dx:
-                        m_copy(4 * dz + dx, ch).start()
+            hops = lambda o: min(o // 4, 8 - o // 4) + min(o % 4, 4 - o % 4)
+            for o in sorted(range(1, 32), key=hops, reverse=True):
+                m_copy(o, ch).start()
 
         begin(
             ("m", ch), far_first,
@@ -473,6 +472,19 @@
         if arrived is not None:
             arrived()
         sent()
+
+
+def hand_over(i_ref, o_ref, v_ref, i_sem, o_sem):
+    parts = [pl.ds(2 * n, 2) for n in range(4)]
+    fetch = [pltpu.make_async_copy(i_ref.at[0, p], v_ref.at[p], i_sem.at[n]) for n, p in enumerate(parts)]
+    store = [pltpu.make_async_copy(v_ref.at[p], o_ref.at[0, p], o_sem.at[n]) for n, p in enumerate(parts)]
+    for copy in fetch:
+        copy.start()
+    for one, two in zip(fetch, store):
+        one.wait()
+        two.start()
+    for copy in store:
+        copy.wait()
 
 
 def solution(mesh):
@@ -522,6 +534,13 @@
             ],
             compiler_params=pltpu.CompilerParams(collective_id=0, has_side_effects=True),
         )(rows, courant_first, courant_second, weights, frame_flip)
+        out = pl.pallas_call(
+            hand_over,
+            out_shape=jax.ShapeDtypeStruct((1, 8, LEV * 8, 128), f32),
+            in_specs=[hbm],
+            out_specs=hbm,
+            scratch_shapes=[pltpu.VMEM((8, LEV * 8, 128), f32), dma((4,)), dma((4,))],
+        )(out)
         return jnp.transpose(out.reshape(1, 8, LEV, 8, 128), (0, 1, 3, 2, 4))
 
     return jax.shard_map(

time: 69.2 us -> 69.1 us (level)
  local copies, waits for them, and re-layouts: 1.92 us -> 0 us
  Pallas kernels: 67.1 us -> 69 us
    unnamed x1 -> x0, local copies, waits for them, and re-layouts: 1.92 us -> none
    pallas_call x0 -> x1, Pallas kernels: none -> 1.85 us  [on_device(): pl.pallas_call(hand_over, out_shape=jax.ShapeDtypeStruct((1, 8, LEV * 8,...]
where the time goes in v7:
time: 69.1 us; the launch traced here: 69 us
  Pallas kernels  69 us (100%)
    pallas_call x1, Pallas kernels, on_device(): pl.pallas_call(kernel, out_shape=jax.ShapeDtypeStruct((1, 8, LEV * 8, 128...  67.1 us
    pallas_call x1, Pallas kernels, on_device(): pl.pallas_call(hand_over, out_shape=jax.ShapeDtypeStruct((1, 8, LEV * 8,...  1.85 us

profile of v7, /device:TPU:41, one launch (start us, length us, event | category | flops | bytes accessed | tf_op | source)
XLA Modules:
  0.0 69.0 jit_solution(5507536100446564330)
XLA Ops:
  0.0 67.1 %shard_map.55.i_ref = f32[1,8,144,128]{3,2,1,0:T(8,128)} custom-call(f32[1,8,18,8,128]{4,3,2,1,0:T(8,128)} %bitcast.4, f32[1,8,8,18]{3,2,1,0:T(8,128)} %c1_ref.1, f32[1,8,8,18]{3,2,1,0:T(8,128)} %c2_ref.1, f32[1,2,8,72,72]{4,3,2,1,0:T(8,128)} %w_ref.1, s32[1,2]{1,0:T(1,128)} %f_ref.1), custom_call_target="tpu_custom_call" | custom-call | tf_op jit(solution)/shard_map/pallas_call | solution.py:497
  67.1 1.9 %shard_map.56 = f32[1,8,144,128]{3,2,1,0:T(8,128)} custom-call(f32[1,8,144,128]{3,2,1,0:T(8,128)} %shard_map.55.i_ref), custom_call_target="tpu_custom_call" | custom-call | tf_op jit(solution)/shard_map/pallas_call | solution.py:537
